TPU v7x, 256 devices: a whole 4x4x8 slice. The times are simulated.
256 devices in a mesh: dp: 128 (over y, z, x), grp: 2 (over core).
Axes of the slice: x: 4, y: 4, z: 8, core: 2. Of those that a mesh axis runs over, the one named last changes fastest.
Arguments:
- embeddings: bfloat16 [65536, 1024], P(('dp', 'grp')), may hold values from -6 to 6
- owner_dest: int32 [65536, 1], P(('dp', 'grp')), may hold values from 0 to 127; in each aligned block of 256 rows (0 to 255, 256 to 511, ...) at most 6 rows name the same one
- cluster_slot: int32 [65536, 1], P(('dp', 'grp')), may hold values from 0 to 7
- cluster_rank: int32 [1024], replicated, may hold values from 0 to 1023, each once
- centroids: bfloat16 [1024, 1024], P('dp'), may hold values from -2 to 2
Outputs:
- shift: bfloat16 [1024, 1792], replicated
- moment: float32 [1024, 256, 256], P(('dp', 'grp'))
Inputs may be any that keep to these rules, and one draw needn't show every extreme that they name: `owner_dest`: among the rows of one device (aligned blocks of 256 rows), no owner is named by more than 6 rows, a bound that some block reaches. `cluster_rank`: A permutation.
All inputs are finite; a program needn't handle non-finite values.
Results may differ from a plain program's by a relative error of at most 0.0034.
Values may be sent and summed in bfloat16 or wider, within the bound.
A program may use at most 64 MiB of HBM per device.

v0:
```python
import jax
import jax.numpy as jnp
from jax import lax
from jax.sharding import PartitionSpec as P

D = 1024
D_SMALL = 256
D_MID = 512


def residuals(rows, cent):
    rows = rows.astype(jnp.float32)
    pieces = []
    for width in (D_SMALL, D_MID, D):
        part = rows[:, :width]
        scale = lax.rsqrt(jnp.mean(part * part, axis=-1, keepdims=True) + 1e-06)
        pieces.append(part * scale - cent[:, :width])
    return jnp.concatenate(pieces, axis=1).astype(jnp.bfloat16)


def slot_onehot(slots, per_owner):
    return (slots[:, None] == jnp.arange(per_owner, dtype=jnp.int32)[None, :]).astype(jnp.bfloat16)


def moments(select, small):
    count_rows = small.shape[0]
    per_owner = select.shape[1]
    spread = (select[:, :, None] * small[:, None, :]).reshape(count_rows, per_owner * D_SMALL)
    gram = jnp.einsum("sa,sb->ab", spread, small, preferred_element_type=jnp.float32)
    return gram.reshape(per_owner, D_SMALL, D_SMALL)


def on_device(embeddings, owner_dest, cluster_slot, cluster_rank, centroids):
    rows_here = embeddings.shape[0]
    width = embeddings.shape[1]
    owners = lax.axis_size("dp")
    per_owner = centroids.shape[0]
    capacity = 3 * rows_here // owners
    dest = owner_dest[:, 0]
    slot = cluster_slot[:, 0]
    hits = (dest[:, None] == jnp.arange(owners, dtype=jnp.int32)[None, :]).astype(jnp.int32)
    before = jnp.cumsum(hits, axis=0) - hits
    position = jnp.sum(before * hits, axis=1)
    target = dest * capacity + position

    def pack(values, fill):
        buffer = jnp.full((owners * capacity,) + values.shape[1:], fill, values.dtype)
        buffer = buffer.at[target].set(values)
        return buffer.reshape((owners, capacity) + values.shape[1:])

    sent_ids = pack(slot, -1)
    sent_rows = pack(embeddings, 0)
    got_rows = lax.all_to_all(sent_rows, "dp", split_axis=0, concat_axis=0, tiled=True)
    got_ids = lax.all_to_all(sent_ids, "dp", split_axis=0, concat_axis=0, tiled=True)
    lead = got_rows.shape[0]
    middle = got_rows.shape[1]
    flat_ids = got_ids.reshape(-1)
    select = slot_onehot(flat_ids, per_owner)
    cent = jnp.dot(select, centroids, preferred_element_type=jnp.float32)
    resid = residuals(got_rows.reshape(-1, width), cent)
    resid, got_ids = (resid.reshape(lead, middle, resid.shape[1]), got_ids)
    resid = resid.reshape(-1, resid.shape[2])
    select = slot_onehot(got_ids.reshape(-1), per_owner)
    sums = jnp.einsum("sc,sw->cw", select, resid, preferred_element_type=jnp.float32)
    counts = jnp.sum(select.astype(jnp.float32), axis=0)
    gram = moments(select, resid[:, :D_SMALL])
    sums_part, counts_part, gram_part = (
        lax.psum_scatter(sums, "grp", scatter_dimension=0, tiled=True),
        lax.psum_scatter(counts, "grp", scatter_dimension=0, tiled=True),
        lax.psum_scatter(gram, "grp", scatter_dimension=0, tiled=True),
    )
    denom = counts_part + 1.0
    table_part = (sums_part / denom[:, None]).astype(jnp.bfloat16)
    table = lax.all_gather(table_part, ("dp", "grp"), axis=0, tiled=True)
    shift = table[cluster_rank]
    moment = gram_part / denom[:, None, None]
    return (shift, moment)


def solution(mesh):
    placed = (
        P(("dp", "grp"), None),
        P(("dp", "grp"), None),
        P(("dp", "grp"), None),
        P(),
        P("dp", None),
    )
    return jax.shard_map(
        on_device,
        mesh=mesh,
        in_specs=placed,
        out_specs=(P(), P(("dp", "grp"), None, None)),
        check_vma=False,
    )
```

profile of v0, /device:TPU:1, one launch (start us, length us, event | category | flops | bytes accessed | tf_op | source)
XLA Modules:
  0.0 256.8 jit_solution(13013240612006386319)
XLA Ops:
  8.0 0.8 copy.12
  9.1 0.9 fusion.18
  10.7 1.6 scatter_custom_fusion
  12.2 0.8 all_to_all.9
  13.0 16.3 %all-to-all-start = ((s32[128,1,6]{2,1,0:T(1,128)}), s32[128,1,6]{2,1,0:T(1,128)S(1)}, u32[]{:S(2)}, u32[]{:S(2)}) async-start(s32[128,1,6]{2,1,0:T(1,128)} %bitcast.8), calls=%async_computation | async-start | bytes 131072 | tf_op jit(solution)/shard_map/all_to_all | solution.py:54
  29.3 2.6 %scatter_custom_fusion.1 = bf16[768,1024]{1,0:T(8,128)(2,1)S(1)} fusion(s32[256]{0:T(256)S(1)} %bitcast.40, bf16[256,1024]{1,0:T(8,128)(2,1)} %param.5, bf16[]{:T(256)} %constant.7.clone.1), kind=kCustom, calls=%fused_computation.22 | custom fusion | bytes 1573376 | tf_op jit(solution)/shard_map/scatter | solution.py:48
  32.0 1.6 reshape.100
  33.5 6.3 %all-to-all-done = s32[128,1,6]{2,1,0:T(1,128)S(1)} async-done(((s32[128,1,6]{2,1,0:T(1,128)}), s32[128,1,6]{2,1,0:T(1,128)S(1)}, u32[]{:S(2)}, u32[]{:S(2)}) %all-to-all-start) | async-done | bytes 3104 | tf_op jit(solution)/shard_map/all_to_all | solution.py:54
  39.8 6.9 %all-to-all-start.1 = ((bf16[128,6,1024]{2,1,0:T(8,128)(2,1)}), bf16[128,6,1024]{2,1,0:T(8,128)(2,1)S(1)}, u32[]{:S(2)}, u32[]{:S(2)}) async-start(bf16[128,6,1024]{2,1,0:T(8,128)(2,1)} %reshape.100), calls=%async_computation.1 | async-start | bytes 4194304 | tf_op jit(solution)/shard_map/all_to_all | solution.py:53
  47.4 0.8 reduce.4
  48.9 47.0 %all-to-all-done.1 = bf16[128,6,1024]{2,1,0:T(8,128)(2,1)S(1)} async-done(((bf16[128,6,1024]{2,1,0:T(8,128)(2,1)}), bf16[128,6,1024]{2,1,0:T(8,128)(2,1)S(1)}, u32[]{:S(2)}, u32[]{:S(2)}) %all-to-all-start.1) | async-done | bytes 1572896 | tf_op jit(solution)/shard_map/all_to_all | solution.py:53
  97.3 2.5 reshape.101
  100.1 1.8 subtract_convert_fusion
  101.9 1.7 copy-done.2
  103.7 0.9 copy.15
  104.7 3.3 %fusion = f32[8,256,256]{2,1,0:T(8,128)} fusion(bf16[768,256]{0,1:T(8,128)(2,1)} %copy.15, bf16[768,8]{0,1:T(8,128)(2,1)} %fusion.22, bf16[768,256]{1,0:T(8,128)(2,1)S(1)} %fusion.12), kind=kOutput, calls=%fused_computation.4 | convolution fusion | flops 806879232 | bytes 2895872 | tf_op jit(solution)/shard_map/sa,sb->ab/dot_general | solution.py:29
  108.1 1.4 dynamic-slice
  109.5 1.3 convert_reduce_fusion
  111.0 1.6 fusion.9
  113.8 7.5 %all-reduce.2 = (f32[8]{0:T(128)S(1)}, f32[8,1792]{1,0:T(8,128)S(1)}) all-reduce(f32[8]{0:T(128)S(1)} %copy-done.7, f32[8,1792]{1,0:T(8,128)S(1)} %fusion.3), channel_id=3, replica_groups=mesh['dp'=128,'grp'=2] {'grp'}, use_global_device_ids=true, to_apply=%region_10.11.clone | all-reduce | flops 14344 | bytes 114752
  122.2 2.4 broadcast_divide_fusion
  124.5 107.6 %all-gather.3.cloned.1.call-done = bf16[256,4,1792]{2,1,0:T(4,128)(2,1)} async-done(((bf16[1,4,1792]{2,1,0:T(4,128)(2,1)}), bf16[256,4,1792]{2,1,0:T(4,128)(2,1)}) %all-gather.3.cloned.1.call-update) | async-done | bytes 3670032 | tf_op jit(solution)/shard_map/all_gather | solution.py:74
  232.1 6.9 %reshape.128 = bf16[1024,1792]{1,0:T(8,128)(2,1)} reshape(bf16[256,4,1792]{2,1,0:T(4,128)(2,1)} %all-gather.3.cloned.1.call-done) | data formatting | bytes 7340032
  238.9 10.4 %gather_fusion = bf16[1024,1792]{1,0:T(8,128)(2,1)} fusion(bf16[1024,1792]{1,0:T(8,128)(2,1)} %reshape.128, s32[1024]{0:T(1024)S(1)} %fusion.27), kind=kCustom, calls=%fused_computation | custom fusion | bytes 7344128 | tf_op jit(solution)/shard_map/gather | solution.py:75
  (43 shorter events, 5.6 us)
Async XLA Ops:
  8.0 92.1 %copy-start = (bf16[8,1024]{1,0:T(8,128)(2,1)S(1)}, bf16[8,1024]{1,0:T(8,128)(2,1)}, u32[]{:S(2)}) copy-start(bf16[8,1024]{1,0:T(8,128)(2,1)} %param.9) | copy-start | bytes 49156
  13.0 26.9 %all-to-all-start = ((s32[128,1,6]{2,1,0:T(1,128)}), s32[128,1,6]{2,1,0:T(1,128)S(1)}, u32[]{:S(2)}, u32[]{:S(2)}) async-start(s32[128,1,6]{2,1,0:T(1,128)} %bitcast.8), calls=%async_computation | async-start | bytes 131072 | tf_op jit(solution)/shard_map/all_to_all | solution.py:54
  39.8 56.0 %all-to-all-start.1 = ((bf16[128,6,1024]{2,1,0:T(8,128)(2,1)}), bf16[128,6,1024]{2,1,0:T(8,128)(2,1)S(1)}, u32[]{:S(2)}, u32[]{:S(2)}) async-start(bf16[128,6,1024]{2,1,0:T(8,128)(2,1)} %reshape.100), calls=%async_computation.1 | async-start | bytes 4194304 | tf_op jit(solution)/shard_map/all_to_all | solution.py:53
  46.8 75.4 %reduce-scatter.2.cloned.1.call-start = ((), (), s32[]{:S(2)}) async-start(), calls=%async_computation.3 | async-start | bytes 3145728 | tf_op jit(solution)/shard_map/reduce_scatter | solution.py:70
  48.3 51.8 %copy-start.4 = (s32[768]{0:T(1024)}, s32[768]{0:T(1024)S(1)}, u32[]{:S(2)}) copy-start(s32[768]{0:T(1024)S(1)} %eq.59) | copy-start | bytes 9220
  95.9 1.3 copy-start.1
  101.9 1.7 copy-start.2
  108.0 124.1 %all-gather.3.cloned.1.call-start = ((), (), s32[]{:S(2)}) async-start(), calls=%async_computation.4 | async-start | bytes 3684352 | tf_op jit(solution)/shard_map/all_gather | solution.py:74
  108.1 4.6 %copy-start.3 = (bf16[768,1024]{1,0:T(8,128)(2,1)S(1)}, bf16[768,1024]{1,0:T(8,128)(2,1)}, u32[]{:S(2)}) copy-start(bf16[768,1024]{1,0:T(8,128)(2,1)} %get-tuple-element.4) | copy-start | bytes 4718596
  108.1 4.6 %copy-start.5 = (s32[768]{0:T(1024)S(1)}, s32[768]{0:T(1024)}, u32[]{:S(2)}) copy-start(s32[768]{0:T(1024)} %copy-done.4) | copy-start | bytes 9220
  112.7 1.1 copy-start.7
  112.7 9.5 %copy-start.6 = (s32[1024]{0:T(1024)S(1)}, s32[1024]{0:T(1024)}, u32[]{:S(2)}) copy-start(s32[1024]{0:T(1024)} %param.8) | copy-start | bytes 12292
Sparse Core Ops, SparseCore 0:
  108.1 13.3 reduce-scatter.1
Sparse Core Ops, SparseCore 1:
  122.2 109.8 all-gather.2
where the time goes:
time: 258 us; the launch traced here: 257 us
  waiting for transfers between devices  161 us (62%)
  local copies, waits for them, and re-layouts  32.7 us (13%)
  starting transfers between devices  23.4 us (9%)
  between operations  16.4 us (6%)
  other arithmetic  10.4 us (4%)
  blocking collectives  7.53 us (3%)
  matrix products  5.58 us (2%)
    all_gather x1, waiting for transfers between devices, on_device(): table = lax.all_gather(table_part, ('dp', 'grp'), axis=0, tiled=True)  108 us
    all_to_all x1, waiting for transfers between devices, on_device(): lax.all_to_all(sent_rows, 'dp', split_axis=0, concat_axis=0, tiled=True)  47 us
    all_to_all x1, starting transfers between devices, on_device(): lax.all_to_all(sent_ids, 'dp', split_axis=0, concat_axis=0, tiled=True)  16.3 us
    unnamed x19, local copies, waits for them, and re-layouts  10.7 us
    gather x1, local copies, waits for them, and re-layouts, on_device(): shift = table[cluster_rank]  10.4 us
    unnamed x1, blocking collectives  7.53 us
    all_to_all x1, starting transfers between devices, on_device(): lax.all_to_all(sent_rows, 'dp', split_axis=0, concat_axis=0, tiled=True)  6.94 us
    all_to_all x1, waiting for transfers between devices, on_device(): lax.all_to_all(sent_ids, 'dp', split_axis=0, concat_axis=0, tiled=True)  6.3 us
  transfers between devices with their start and end apart: 4, of which 3 were waited for; matrix products, arithmetic and copies ran while one was open for 6% of the time, Pallas kernels for 0%

commit v1 on v0

--- a/solution.py
+++ b/solution.py
@@ -1,11 +1,19 @@
+import functools
+
 import jax
 import jax.numpy as jnp
 from jax import lax
+from jax.experimental import pallas as pl
+from jax.experimental.pallas import tpu as pltpu
 from jax.sharding import PartitionSpec as P
 
 D = 1024
 D_SMALL = 256
 D_MID = 512
+WIDE = 1792
+HALF = 896
+NX, NY, NZ = 4, 4, 8
+MESH = pl.DeviceIdType.MESH
 
 
 def residuals(rows, cent):
@@ -28,6 +36,134 @@
     spread = (select[:, :, None] * small[:, None, :]).reshape(count_rows, per_owner * D_SMALL)
     gram = jnp.einsum("sa,sb->ab", spread, small, preferred_element_type=jnp.float32)
     return gram.reshape(per_owner, D_SMALL, D_SMALL)
+
+
+def gather_table(blk_ref, out_ref, own_sem, zs, zr, as_, ar, ps, pr):
+    dp = lax.axis_index("dp")
+    g = lax.axis_index("grp")
+    x = dp % NX
+    z = (dp // NX) % NZ
+    y = dp // (NX * NZ)
+    h = 1 - g
+
+    def dev(yy, zz, xx, gg):
+        return ((yy * NZ + zz) * NX + xx, gg)
+
+    def place(i, j):
+        return (y + 4 + i * g + j * h) % NY, (x + 4 + i * h + j * g) % NX
+
+    cols = pl.ds(pl.multiple_of(g * HALF, 128), HALF)
+    pcols = pl.ds(pl.multiple_of(h * HALF, 128), HALF)
+
+    def chunk(i, j, z0=0, nz=NZ, at=cols):
+        yy, xx = place(i, j)
+        return out_ref.at[yy, pl.ds(z0, nz), xx, :, at]
+
+    def to(i, j):
+        yy, xx = place(i, j)
+        return dev(yy, z, xx, g)
+
+    partner = dev(y, z, x, h)
+    zpeers = [dev(y, (z + d) % NZ, x, g) for d in range(1, NZ)]
+    barrier = pltpu.get_barrier_semaphore()
+    peers = zpeers + [to(1, 0), to(-1, 0), to(0, 1), to(0, -1), partner]
+    for peer in peers:
+        pl.semaphore_signal(barrier, inc=1, device_id=peer, device_id_type=MESH)
+    pl.semaphore_wait(barrier, len(peers))
+
+    sent = []
+
+    def send(src, dst, ss, rs, peer):
+        c = pltpu.make_async_remote_copy(src_ref=src, dst_ref=dst, send_sem=ss, recv_sem=rs,
+                                         device_id=peer, device_id_type=MESH)
+        c.start()
+        sent.append(c)
+        return c
+
+    mine = out_ref.at[y, z, x, :, cols]
+    zc = []
+    for d in range(1, NZ):
+        zc.append(send(blk_ref, mine, zs.at[d - 1], zr.at[d - 1], zpeers[d - 1]))
+    own = pltpu.make_async_copy(blk_ref, mine, own_sem)
+    own.start()
+    own.wait()
+
+    def got(ref, sem):
+        pltpu.make_async_copy(ref, ref, sem).wait()
+
+    for d in range(1, NZ):
+        got(mine, zr.at[d - 1])
+
+    order = [0, -1, 1, 2]
+    pn = [0]
+    partner_chunks = []
+
+    def share(i, j):
+        k = pn[0]
+        pn[0] += 1
+        send(chunk(i, j), chunk(i, j), ps.at[k], pr.at[k], partner)
+
+    def ring_out(row, here, plus, minus):
+        send(here, here, as_.at[row, 0], ar.at[row, 0], plus)
+        send(here, here, as_.at[row, 1], ar.at[row, 1], minus)
+
+    def first(i):
+        return to(1, 0) if i > 0 else to(-1, 0)
+
+    ring_out(0, chunk(0, 0), to(1, 0), to(-1, 0))
+    ring_out(1, chunk(0, 0), to(0, 1), to(0, -1))
+    share(0, 0)
+    got(chunk(-1, 0), ar.at[0, 0])
+    low = chunk(-1, 0, 0, 4)
+    send(low, low, as_.at[0, 2], ar.at[0, 2], to(1, 0))
+    ring_out(2, chunk(-1, 0), to(0, 1), to(0, -1))
+    share(-1, 0)
+    got(chunk(1, 0), ar.at[0, 1])
+    high = chunk(1, 0, 4, 4)
+    send(high, high, as_.at[0, 3], ar.at[0, 3], to(-1, 0))
+    ring_out(3, chunk(1, 0), to(0, 1), to(0, -1))
+    share(1, 0)
+
+    def second(row, i):
+        got(chunk(i, -1), ar.at[row, 0])
+        lo = chunk(i, -1, 0, 4)
+        send(lo, lo, as_.at[row, 2], ar.at[row, 2], to(0, 1))
+        share(i, -1)
+        got(chunk(i, 1), ar.at[row, 1])
+        hi = chunk(i, 1, 4, 4)
+        send(hi, hi, as_.at[row, 3], ar.at[row, 3], to(0, -1))
+        share(i, 1)
+
+    second(1, 0)
+    got(chunk(2, 0, 0, 4), ar.at[0, 2])
+    got(chunk(2, 0, 4, 4), ar.at[0, 3])
+    ring_out(4, chunk(2, 0), to(0, 1), to(0, -1))
+    share(2, 0)
+    second(2, -1)
+    second(3, 1)
+    second(4, 2)
+    for row, i in ((1, 0), (2, -1), (3, 1), (4, 2)):
+        got(chunk(i, 2, 0, 4), ar.at[row, 2])
+        got(chunk(i, 2, 4, 4), ar.at[row, 3])
+        share(i, 2)
+    for k in range(16):
+        got(chunk(0, 0, at=pcols), pr.at[k])
+    for c in sent:
+        c.wait_send()
+
+
+def all_tables(block):
+    dma = pltpu.SemaphoreType.DMA
+    out = pl.pallas_call(
+        gather_table,
+        out_shape=jax.ShapeDtypeStruct((NY, NZ, NX, 8, WIDE), jnp.bfloat16),
+        in_specs=[pl.BlockSpec(memory_space=pltpu.VMEM)],
+        out_specs=pl.BlockSpec(memory_space=pltpu.VMEM),
+        scratch_shapes=[dma, dma((7,)), dma((7,)), dma((5, 4)), dma((5, 4)), dma((16,)), dma((16,))],
+        compiler_params=pltpu.CompilerParams(collective_id=1, has_side_effects=True),
+        name="gather_table",
+    )(block)
+    return out.reshape(NY * NZ * NX * 8, WIDE)
 
 
 def on_device(embeddings, owner_dest, cluster_slot, cluster_rank, centroids):
@@ -52,28 +188,24 @@
     sent_rows = pack(embeddings, 0)
     got_rows = lax.all_to_all(sent_rows, "dp", split_axis=0, concat_axis=0, tiled=True)
     got_ids = lax.all_to_all(sent_ids, "dp", split_axis=0, concat_axis=0, tiled=True)
-    lead = got_rows.shape[0]
-    middle = got_rows.shape[1]
     flat_ids = got_ids.reshape(-1)
     select = slot_onehot(flat_ids, per_owner)
     cent = jnp.dot(select, centroids, preferred_element_type=jnp.float32)
     resid = residuals(got_rows.reshape(-1, width), cent)
-    resid, got_ids = (resid.reshape(lead, middle, resid.shape[1]), got_ids)
-    resid = resid.reshape(-1, resid.shape[2])
-    select = slot_onehot(got_ids.reshape(-1), per_owner)
     sums = jnp.einsum("sc,sw->cw", select, resid, preferred_element_type=jnp.float32)
     counts = jnp.sum(select.astype(jnp.float32), axis=0)
     gram = moments(select, resid[:, :D_SMALL])
-    sums_part, counts_part, gram_part = (
-        lax.psum_scatter(sums, "grp", scatter_dimension=0, tiled=True),
-        lax.psum_scatter(counts, "grp", scatter_dimension=0, tiled=True),
-        lax.psum_scatter(gram, "grp", scatter_dimension=0, tiled=True),
-    )
-    denom = counts_part + 1.0
+    counts = lax.psum(counts, "grp")
+    sums_part = lax.psum_scatter(sums, "grp", scatter_dimension=1, tiled=True)
+    gram_part = lax.psum_scatter(gram, "grp", scatter_dimension=0, tiled=True)
+    denom = counts + 1.0
     table_part = (sums_part / denom[:, None]).astype(jnp.bfloat16)
-    table = lax.all_gather(table_part, ("dp", "grp"), axis=0, tiled=True)
-    shift = table[cluster_rank]
-    moment = gram_part / denom[:, None, None]
+    table = all_tables(table_part)
+    pick = (cluster_rank[:, None] == jnp.arange(table.shape[0], dtype=jnp.int32)[None, :]).astype(jnp.bfloat16)
+    shift = jnp.dot(pick, table, preferred_element_type=jnp.float32).astype(jnp.bfloat16)
+    g = lax.axis_index("grp")
+    mine = lax.dynamic_slice_in_dim(denom, g * (per_owner // 2), per_owner // 2, 0)
+    moment = gram_part / mine[:, None, None]
     return (shift, moment)
 
 

time: 258 us -> 170 us (0.66)
  waiting for transfers between devices: 161 us -> 55.2 us
  Pallas kernels: 0 us -> 32.2 us
  local copies, waits for them, and re-layouts: 32.7 us -> 10.9 us
  matrix products: 5.58 us -> 14.6 us
    all_gather x1 -> x0, waiting for transfers between devices: 108 us -> none  [on_device(): table = lax.all_gather(table_part, ('dp', 'grp'), axis=0, tiled=True)]
    pallas_call x0 -> x1, Pallas kernels: none -> 32.2 us  [all_tables(): pl.pallas_call(gather_table, out_shape=jax.ShapeDtypeStruct((NY, NZ, NX,...]
    unnamed x19 -> x11, local copies, waits for them, and re-layouts: 10.7 us -> 0.03 us
    gather x1 -> x0, local copies, waits for them, and re-layouts: 10.4 us -> none  [on_device(): shift = table[cluster_rank]]
    dot_general x0 -> x1, matrix products: none -> 7.72 us  [on_device(): jnp.dot(pick, table, preferred_element_type=jnp.float32)]
    unnamed x1 -> x0, blocking collectives: 7.53 us -> none
    psum x0 -> x1, blocking collectives: none -> 6.71 us  [on_device(): counts = lax.psum(counts, 'grp')]
  transfers between devices with their start and end apart: 4 -> 4, of which waited for: 3 -> 3; matrix products, arithmetic and copies ran while one was open for 6% -> 11% of each run, Pallas kernels for 0% -> 19%
where the time goes in v1:
time: 170 us; the launch traced here: 169 us
  waiting for transfers between devices  55.2 us (32%)
  Pallas kernels  32.2 us (19%)
  starting transfers between devices  23.9 us (14%)
  matrix products  14.6 us (9%)
  between operations  14.3 us (8%)
  other arithmetic  11.1 us (7%)
  local copies, waits for them, and re-layouts  10.9 us (6%)
  blocking collectives  6.71 us (4%)
    all_to_all x1, waiting for transfers between devices, on_device(): lax.all_to_all(sent_rows, 'dp', split_axis=0, concat_axis=0, tiled=True)  46.3 us
    pallas_call x1, Pallas kernels, all_tables(): pl.pallas_call(gather_table, out_shape=jax.ShapeDtypeStruct((NY, NZ, NX,...  32.2 us
    all_to_all x1, starting transfers between devices, on_device(): lax.all_to_all(sent_ids, 'dp', split_axis=0, concat_axis=0, tiled=True)  16.3 us
    dot_general x1, matrix products, on_device(): jnp.dot(pick, table, preferred_element_type=jnp.float32)  7.72 us
    all_to_all x1, starting transfers between devices, on_device(): lax.all_to_all(sent_rows, 'dp', split_axis=0, concat_axis=0, tiled=True)  7.47 us
    psum x1, blocking collectives, on_device(): counts = lax.psum(counts, 'grp')  6.71 us
    all_to_all x1, waiting for transfers between devices, on_device(): lax.all_to_all(sent_ids, 'dp', split_axis=0, concat_axis=0, tiled=True)  6.3 us
    scatter x2, local copies, waits for them, and re-layouts, pack(): buffer = buffer.at[target].set(values)  4.18 us
  transfers between devices with their start and end apart: 4, of which 3 were waited for; matrix products, arithmetic and copies ran while one was open for 11% of the time, Pallas kernels for 19%

profile of v1, /device:TPU:1, one launch (start us, length us, event | category | flops | bytes accessed | tf_op | source)
XLA Modules:
  0.0 168.8 jit_solution(1763111008427489325)
XLA Ops:
  7.2 0.8 copy.12
  8.3 0.9 fusion.21
  9.1 0.7 compare_select_fusion
  9.8 1.6 scatter_custom_fusion
  11.4 0.8 all_to_all.9
  12.2 16.3 %all-to-all-start = ((s32[128,1,6]{2,1,0:T(1,128)}), s32[128,1,6]{2,1,0:T(1,128)S(1)}, u32[]{:S(2)}, u32[]{:S(2)}) async-start(s32[128,1,6]{2,1,0:T(1,128)} %bitcast.8), calls=%async_computation | async-start | bytes 131072 | tf_op jit(solution)/shard_map/all_to_all | solution.py:190
  28.5 2.6 %scatter_custom_fusion.1 = bf16[768,1024]{1,0:T(8,128)(2,1)S(1)} fusion(s32[256]{0:T(256)S(1)} %bitcast.40, bf16[256,1024]{1,0:T(8,128)(2,1)} %param.5, bf16[]{:T(256)} %constant.8.clone.1), kind=kCustom, calls=%fused_computation.25 | custom fusion | bytes 1573376 | tf_op jit(solution)/shard_map/scatter | solution.py:184
  31.1 1.6 reshape.104
  32.7 6.3 %all-to-all-done = s32[128,1,6]{2,1,0:T(1,128)S(1)} async-done(((s32[128,1,6]{2,1,0:T(1,128)}), s32[128,1,6]{2,1,0:T(1,128)S(1)}, u32[]{:S(2)}, u32[]{:S(2)}) %all-to-all-start) | async-done | bytes 3104 | tf_op jit(solution)/shard_map/all_to_all | solution.py:190
  39.0 7.5 %all-to-all-start.1 = ((bf16[128,6,1024]{2,1,0:T(8,128)(2,1)}), bf16[128,6,1024]{2,1,0:T(8,128)(2,1)}, u32[]{:S(2)}, u32[]{:S(2)}) async-start(bf16[128,6,1024]{2,1,0:T(8,128)(2,1)} %reshape.104), calls=%async_computation.1 | async-start | bytes 4194304 | tf_op jit(solution)/shard_map/all_to_all | solution.py:189
  47.1 0.8 reduce.4
  48.6 46.3 %all-to-all-done.1 = bf16[128,6,1024]{2,1,0:T(8,128)(2,1)} async-done(((bf16[128,6,1024]{2,1,0:T(8,128)(2,1)}), bf16[128,6,1024]{2,1,0:T(8,128)(2,1)}, u32[]{:S(2)}, u32[]{:S(2)}) %all-to-all-start.1) | async-done | bytes 1572896 | tf_op jit(solution)/shard_map/all_to_all | solution.py:189
  94.9 2.5 %reshape.106 = f32[768,1024]{1,0:T(8,128)S(1)} reshape(bf16[128,6,1024]{2,1,0:T(8,128)(2,1)} %all-to-all-done.1) | data formatting | bytes 4718592 | tf_op jit(solution)/shard_map/convert_element_type | solution.py:20
  97.9 2.2 %multiply_reduce_fusion = f32[128,6]{1,0:T(8,128)S(1)} fusion(bf16[128,6,1024]{2,1,0:T(8,128)(2,1)} %all-to-all-done.1), kind=kLoop, calls=%fused_computation.2 | loop fusion | flops 2358528 | bytes 1575936 | tf_op jit(solution)/shard_map/reduce_sum | solution.py:24
  100.3 1.8 %subtract_convert_fusion = (bf16[768,1024]{1,0:T(8,128)(2,1)}, f32[768,1024]{1,0:T(8,128)S(1)}) fusion(f32[768,1024]{1,0:T(8,128)S(1)} %reshape.106, f32[768]{0:T(1024)S(1)} %rsqrt.30, bf16[8,1024]{1,0:T(8,128)(2,1)S(1)} %copy-done, s32[768]{0:T(1024)S(1)} %eq.68), kind=kOutput, calls=%fused_computation.9 | convolution fusion | flops 14948352 | bytes 7886848 | tf_op jit(solution)/shard_map/dot_general | solution.py:193
  102.0 1.2 fusion.12
  103.6 2.7 %fusion.5 = f32[8,1792]{1,0:T(8,128)} fusion(bf16[768,1024]{1,0:T(8,128)(2,1)} %get-tuple-element.2, bf16[768,512]{1,0:T(8,128)(2,1)} %fusion.12, bf16[768,256]{1,0:T(8,128)(2,1)S(1)} %fusion.15, s32[768]{0:T(1024)} %copy-done.1), kind=kOutput, calls=%fused_computation.10 | convolution fusion | flops 30283776 | bytes 2812928 | tf_op jit(solution)/shard_map/sc,sw->cw/dot_general | solution.py:195
  106.4 2.3 %fusion.2 = f32[8,256,256]{2,1,0:T(8,128)} fusion(bf16[768,256]{0,1:T(8,128)(2,1)S(1)} %copy.15, bf16[768,8]{0,1:T(8,128)(2,1)S(1)} %copy-done.3, bf16[768,256]{1,0:T(8,128)(2,1)S(1)} %fusion.15), kind=kOutput, calls=%fused_computation.6 | convolution fusion | flops 806879232 | bytes 2895872 | tf_op jit(solution)/shard_map/sa,sb->ab/dot_general | solution.py:37
  108.9 6.7 %psum.7 = f32[8]{0:T(128)S(1)} all-reduce(f32[8]{0:T(128)S(1)} %convert_reduce_fusion), channel_id=1, replica_groups=mesh['dp'=128,'grp'=2] {'grp'}, use_global_device_ids=true, to_apply=%region_10.11 | all-reduce | flops 8 | bytes 64 | tf_op jit(solution)/shard_map/psum | solution.py:198
  115.7 2.6 %reduce-scatter.3.cloned.1.call-done = f32[8,896]{1,0:T(8,128)} async-done(((f32[8,1792]{1,0:T(8,128)}), f32[8,896]{1,0:T(8,128)}) %reduce-scatter.3.cloned.1.call-update) | async-done | bytes 28688 | tf_op jit(solution)/shard_map/reduce_scatter | solution.py:199
  118.3 1.4 divide_convert_fusion.blk_ref
  119.7 32.2 %gather_table.1 = bf16[4,8,4,8,1792]{4,3,2,1,0:T(8,128)(2,1)} custom-call(bf16[8,896]{1,0:T(8,128)(2,1)} %divide_convert_fusion.blk_ref), custom_call_target="tpu_custom_call" | custom-call | tf_op jit(solution)/shard_map/gather_table/pallas_call | solution.py:157
  151.9 7.7 %fusion.1 = bf16[1024,1792]{1,0:T(8,128)(2,1)} fusion(bf16[1024,1792]{1,0:T(8,128)(2,1)} %bitcast.32, s32[1024]{0:T(1024)S(1)} %copy-done.4), kind=kOutput, calls=%fused_computation.5 | convolution fusion | flops 3760979968 | bytes 7344128 | tf_op jit(solution)/shard_map/dot_general | solution.py:205
  159.6 2.4 %broadcast_divide_fusion = f32[4,256,256]{2,1,0:T(8,128)} fusion(f32[4,256,256]{2,1,0:T(8,128)} %reduce-scatter.5.cloned.1.call-done, f32[4]{0:T(128)S(1)} %dynamic_slice.3), kind=kLoop, calls=%fused_computation.27 | loop fusion | flops 262144 | bytes 2097168 | tf_op jit(solution)/shard_map/div | solution.py:208
  (36 shorter events, 2.7 us)
Async XLA Ops:
  7.2 93.1 %copy-start = (bf16[8,1024]{1,0:T(8,128)(2,1)S(1)}, bf16[8,1024]{1,0:T(8,128)(2,1)}, u32[]{:S(2)}) copy-start(bf16[8,1024]{1,0:T(8,128)(2,1)} %param.9) | copy-start | bytes 49156
  12.2 26.9 %all-to-all-start = ((s32[128,1,6]{2,1,0:T(1,128)}), s32[128,1,6]{2,1,0:T(1,128)S(1)}, u32[]{:S(2)}, u32[]{:S(2)}) async-start(s32[128,1,6]{2,1,0:T(1,128)} %bitcast.8), calls=%async_computation | async-start | bytes 131072 | tf_op jit(solution)/shard_map/all_to_all | solution.py:190
  39.0 55.9 %all-to-all-start.1 = ((bf16[128,6,1024]{2,1,0:T(8,128)(2,1)}), bf16[128,6,1024]{2,1,0:T(8,128)(2,1)}, u32[]{:S(2)}, u32[]{:S(2)}) async-start(bf16[128,6,1024]{2,1,0:T(8,128)(2,1)} %reshape.104), calls=%async_computation.1 | async-start | bytes 4194304 | tf_op jit(solution)/shard_map/all_to_all | solution.py:189
  46.5 71.8 %reduce-scatter.3.cloned.1.call-start = ((), (), s32[]{:S(2)}) async-start(), calls=%async_computation.4 | async-start | bytes 86016 | tf_op jit(solution)/shard_map/reduce_scatter | solution.py:199
  48.0 52.2 %copy-start.1 = (s32[768]{0:T(1024)}, s32[768]{0:T(1024)S(1)}, u32[]{:S(2)}) copy-start(s32[768]{0:T(1024)S(1)} %eq.68) | copy-start | bytes 9220
  103.6 2.8 %copy-start.3 = (bf16[768,8]{0,1:T(8,128)(2,1)S(1)}, bf16[768,8]{0,1:T(8,128)(2,1)}, u32[]{:S(2)}) copy-start(bf16[768,8]{0,1:T(8,128)(2,1)} %fusion.24) | copy-start | bytes 36868
  106.3 2.4 %copy-start.2 = (s32[768]{0:T(1024)S(1)}, s32[768]{0:T(1024)}, u32[]{:S(2)}) copy-start(s32[768]{0:T(1024)} %copy-done.1) | copy-start | bytes 9220
  106.3 53.3 %reduce-scatter.5.cloned.1.call-start = ((), (), s32[]{:S(2)}) async-start(), calls=%async_computation.5 | async-start | bytes 3145728 | tf_op jit(solution)/shard_map/reduce_scatter | solution.py:200
  108.7 43.2 %copy-start.4 = (s32[1024]{0:T(1024)S(1)}, s32[1024]{0:T(1024)}, u32[]{:S(2)}) copy-start(s32[1024]{0:T(1024)} %param.8) | copy-start | bytes 12292
Sparse Core Ops, SparseCore 0:
  106.5 11.7 reduce-scatter.2
  120.8 15.8 reduce-scatter.4

commit v2 on v1

v2 whole, which is shorter than its diff:
```python
import functools

import jax
import jax.numpy as jnp
from jax import lax
from jax.experimental import pallas as pl
from jax.experimental.pallas import tpu as pltpu
from jax.sharding import PartitionSpec as P

WIDE = 1792
HALF = 896
NX, NY, NZ = 4, 4, 8
CHIPS = 128
SM = 256
MESH = pl.DeviceIdType.MESH
F32 = jnp.float32
BF16 = jnp.bfloat16
EPS = 1e-06


def iota(shape, dim):
    return lax.broadcasted_iota(jnp.int32, shape, dim)


def thirds(v):
    hi = v.astype(BF16)
    rest = v - hi.astype(F32)
    mid = rest.astype(BF16)
    return hi, mid, (rest - mid.astype(F32)).astype(BF16)


def row_of(col):
    n = col.shape[0]
    eye = iota((n, n), 0) == iota((n, n), 1)
    return jnp.sum(jnp.where(eye, col, 0.0), axis=0, keepdims=True)


def scales(rows):
    sq = rows * rows
    s512 = jnp.sum(sq[:, :512], axis=1, keepdims=True)
    s1024 = s512 + jnp.sum(sq[:, 512:], axis=1, keepdims=True)
    return lax.rsqrt(s512 * (1.0 / 512) + EPS), lax.rsqrt(s1024 * (1.0 / 1024) + EPS)


def pack(emb_ref, dest_ref, slot_ref, sendbuf):
    n = emb_ref.shape[0]
    dest = dest_ref[...]
    slot = slot_ref[...]
    destf = dest.astype(F32)
    hits = dest == iota((n, CHIPS), 1)
    lower = (iota((n, n), 1) < iota((n, n), 0)).astype(BF16)
    before = jnp.dot(lower, hits.astype(F32).astype(BF16), preferred_element_type=F32)
    pos = jnp.sum(jnp.where(hits, before, 0.0), axis=1, keepdims=True)
    target = row_of(destf * 8.0 + pos).astype(jnp.int32)
    destrow = row_of(destf).astype(jnp.int32)
    s512, s1024 = scales(emb_ref[...].astype(F32))
    values = [slot.astype(F32) + 1.0]
    for s in (s512, s1024):
        values += [t.astype(F32) for t in thirds(s)]
    lane = iota((n, 128), 1)
    tags = jnp.zeros((n, 128), F32)
    for q, v in enumerate(values):
        tags = jnp.where((lane & 15) == q, v, tags)
    tags = jnp.where((lane >> 4) == pos.astype(jnp.int32), tags, 0.0).astype(BF16)
    owner = (iota((CHIPS, n), 0) == destrow).astype(F32).astype(BF16)
    tags = jnp.dot(owner, tags, preferred_element_type=F32)
    place = (iota((CHIPS * 8, n), 0) == target).astype(F32).astype(BF16)
    rows = jnp.dot(place, emb_ref[:, :SM], preferred_element_type=F32).reshape(CHIPS, 8, SM)
    wide = jnp.concatenate([tags, jnp.zeros((CHIPS, SM - 128), F32)], axis=1)
    rows = jnp.where(iota((CHIPS, 8, SM), 1) == 6, wide[:, None, :], rows)
    sendbuf[...] = rows.astype(BF16)


def whole(embs, dests, slots, g, total):
    hots, las, lbs = [], [], []
    for emb_ref, dest_ref, slot_ref in zip(embs, dests, slots):
        dest = dest_ref[...]
        xx, zz, yy = dest & 3, (dest >> 2) & 7, dest >> 5
        a = xx * (1 - g) + yy * g
        b = yy * (1 - g) + xx * g
        order = ((a * 4 + b) * 8 + zz) * 8 + slot_ref[...]
        hots.append(row_of(order.astype(F32)))
        s512, s1024 = scales(emb_ref[...].astype(F32))
        gf = g.astype(F32)
        sa = s512 * (1.0 - gf) + s1024 * gf
        ca = pl.ds(pl.multiple_of(256 + g * 256, 256), 256)
        cb = pl.ds(pl.multiple_of(256 + g * 512, 256), 256)
        las.append(thirds(emb_ref[:, ca].astype(F32) * sa))
        lbs.append(thirds(emb_ref[:, cb].astype(F32) * s1024))
    order = jnp.concatenate(hots, axis=1).astype(jnp.int32)
    k = 8 * CHIPS
    hot = (iota((k, order.shape[1]), 0) == order).astype(F32).astype(BF16)
    for at, parts in ((0, las), (256, lbs)):
        acc = jnp.zeros((k, 256), F32)
        for t in range(3):
            x = jnp.concatenate([p[t] for p in parts], axis=0)
            acc = acc + jnp.dot(hot, x, preferred_element_type=F32)
        total[:, :, :, :, at:at + 256] = acc.reshape(4, 4, NZ, 8, 256)


def routed(emb_ref, dest_ref, slot_ref, cent_ref, table_ref, gram_ref,
           sendbuf, recvbuf, pemb, pdest, pslot, total, half1, full1, half2, full2, zgot, blk, psums, osums,
           pgram, ogram,
           own_sem, a2s, a2r, xs, xr, r1s, r1r, r2s, r2r, z3s, z3r, pss, psr, pgs, pgr,
           zs, zr, as_, ar, ps, pr):
    dp = lax.axis_index("dp")
    g = lax.axis_index("grp")
    x = dp % NX
    z = (dp // NX) % NZ
    y = dp // (NX * NZ)
    h = 1 - g
    partner = (dp, h)
    barrier = pltpu.get_barrier_semaphore()
    pl.semaphore_signal(barrier, inc=1, device_id=partner, device_id_type=MESH)

    def chip(d):
        return (((y + d // 32) % NY) * NZ + (z + (d // 4) % NZ) % NZ) * NX + (x + d % 4) % NX

    def greet(d, c):
        pl.semaphore_signal(barrier, inc=1, device_id=(chip(d), g), device_id_type=MESH)
        return c

    lax.fori_loop(1, CHIPS, greet, 0)
    pack(emb_ref, dest_ref, slot_ref, sendbuf)
    pl.semaphore_wait(barrier, CHIPS)

    sent = []

    def send(src, dst, ss, rs, peer):
        c = pltpu.make_async_remote_copy(src_ref=src, dst_ref=dst, send_sem=ss, recv_sem=rs,
                                         device_id=peer, device_id_type=MESH)
        c.start()
        sent.append(c)

    def got(ref, sem):
        pltpu.make_async_copy(ref, ref, sem).wait()

    send(emb_ref, pemb, xs.at[0], xr.at[0], partner)
    send(dest_ref, pdest, xs.at[1], xr.at[1], partner)
    send(slot_ref, pslot, xs.at[2], xr.at[2], partner)
    mine = pltpu.make_async_copy(sendbuf.at[dp], recvbuf.at[dp], own_sem.at[0])
    mine.start()

    def scatter(d, c):
        t = chip(d)
        pltpu.make_async_remote_copy(src_ref=sendbuf.at[t], dst_ref=recvbuf.at[dp], send_sem=a2s, recv_sem=a2r,
                                     device_id=(t, g), device_id_type=MESH).start()
        return c

    lax.fori_loop(1, CHIPS, scatter, 0)
    got(pemb, xr.at[0])
    got(pdest, xr.at[1])
    got(pslot, xr.at[2])
    whole((emb_ref, pemb), (dest_ref, pdest), (slot_ref, pslot), g, total)

    def to(i, j):
        yy, xx = (y + 4 + i * g + j * h) % NY, (x + 4 + i * h + j * g) % NX
        return ((yy * NZ + z) * NX + xx, g)

    p = x * h + y * g
    q = y * h + x * g

    def ring(at, me, lo, hi, half, full, plus, minus, ss, rs):
        up, down, far = (me + 1) % 4, (me + 3) % 4, (me + 2) % 4
        send(at(far, lo), half.at[0], ss.at[0], rs.at[0], plus)
        send(at(far, hi), half.at[1], ss.at[1], rs.at[1], minus)
        send(at(up, hi), full.at[0, hi], ss.at[2], rs.at[2], plus)
        send(at(down, lo), full.at[1, lo], ss.at[3], rs.at[3], minus)
        got(half.at[0], rs.at[0])
        ref = at(up, lo)
        ref[...] = ref[...] + half[0]
        send(ref, full.at[0, lo], ss.at[4], rs.at[4], plus)
        got(half.at[1], rs.at[1])
        ref = at(down, hi)
        ref[...] = ref[...] + half[1]
        send(ref, full.at[1, hi], ss.at[5], rs.at[5], minus)
        got(full.at[0, hi], rs.at[2])
        got(full.at[1, lo], rs.at[3])
        got(full.at[0, lo], rs.at[4])
        got(full.at[1, hi], rs.at[5])
        for part in (lo, hi):
            ref = at(me, part)
            ref[...] = ref[...] + full[0, part] + full[1, part]

    ring(lambda i, s: total.at[i, s], p, pl.ds(0, 2), pl.ds(2, 2), half1, full1, to(1, 0), to(-1, 0), r1s, r1r)
    ring(lambda i, s: total.at[p, i, s], q, pl.ds(0, 4), pl.ds(4, 4), half2, full2, to(0, 1), to(0, -1), r2s, r2r)

    def along_z(d):
        return ((y * NZ + (z + d) % NZ) * NX + x, g)

    for d in range(1, NZ):
        send(total.at[p, q, (z + d) % NZ], zgot.at[d - 1], z3s.at[d - 1], z3r.at[d - 1], along_z(d))

    mine.wait()
    every = recvbuf.at[pl.ds(0, CHIPS - 1)]
    got(every, a2r)
    rows = recvbuf[...].astype(F32)
    slots = CHIPS * 8
    tags = jnp.broadcast_to(rows[:, 6:7, :128], (CHIPS, 8, 128)).reshape(slots, 128)
    lane = iota((slots, 128), 1)
    tags = jnp.where((lane >> 4) == (iota((slots, 128), 0) & 7), tags, 0.0).astype(BF16)
    f = iota((128, 128), 0) & 15
    c = iota((128, 128), 1)
    pick = ((f == 0) & (c == 0)) | ((f >= 1) & (f <= 3) & (c == 1)) | ((f >= 4) & (f <= 6) & (c == 2))
    vals = jnp.dot(tags, pick.astype(F32).astype(BF16), preferred_element_type=F32)
    idrow = vals.T[0:1, :]
    selt = (idrow == (iota((8, slots), 0) + 1).astype(F32)).astype(F32)
    sel = (vals[:, 0:1] == (iota((slots, 8), 1) + 1).astype(F32)).astype(F32).astype(BF16)
    cent = jnp.dot(sel, cent_ref[:, :SM], preferred_element_type=F32)
    rows = rows.reshape(slots, SM)
    s256 = lax.rsqrt(jnp.sum(rows * rows, axis=1, keepdims=True) * (1.0 / 256) + EPS)
    small = (rows * s256 - cent).astype(BF16)
    seltb = selt.astype(BF16)
    osums[:, 0:256] = jnp.dot(seltb, small, preferred_element_type=F32)
    osums[:, 256:512] = jnp.dot(seltb, (rows * vals[:, 1:2] - cent).astype(BF16), preferred_element_type=F32)
    osums[:, 512:768] = jnp.dot(seltb, (rows * vals[:, 2:3] - cent).astype(BF16), preferred_element_type=F32)
    osums[:, 768:896] = jnp.broadcast_to(jnp.sum(selt, axis=1, keepdims=True), (8, 128))
    send(osums, psums, pss, psr, partner)
    smallt = small.astype(F32).T

    def gram(c):
        keep = idrow == (c + 1).astype(F32)
        return jnp.dot(jnp.where(keep, smallt, 0.0).astype(BF16), small, preferred_element_type=F32)

    for d in range(1, NZ):
        got(zgot.at[d - 1], z3r.at[d - 1])
    got(psums, psr)
    sums = osums[...] + psums[...]
    count = sums[:, 768:769]
    denom = count + 1.0
    big = total[p, q, z]
    for d in range(1, NZ):
        big = big + zgot[d - 1]
    ca = pl.ds(pl.multiple_of(256 + g * 256, 256), 256)
    cb = pl.ds(pl.multiple_of(256 + g * 512, 256), 256)
    blk[:, 0:256] = ((big[:, :256] - count * cent_ref[:, ca].astype(F32)) / denom).astype(BF16)
    blk[:, 256:512] = ((big[:, 256:] - count * cent_ref[:, cb].astype(F32)) / denom).astype(BF16)
    gf = g.astype(F32)
    part = jnp.where(gf > 0.5, sums[:, 384:768], sums[:, 0:384])
    blk[:, 512:896] = (part / denom).astype(BF16)

    cols = pl.ds(pl.multiple_of(g * HALF, 128), HALF)
    pcols = pl.ds(pl.multiple_of(h * HALF, 128), HALF)

    def chunk(i, j, z0=0, nz=NZ, at=cols):
        yy, xx = (y + 4 + i * g + j * h) % NY, (x + 4 + i * h + j * g) % NX
        return table_ref.at[yy, pl.ds(z0, nz), xx, :, at]

    home = table_ref.at[y, z, x, :, cols]
    for d in range(1, NZ):
        send(blk, home, zs.at[d - 1], zr.at[d - 1], along_z(d))
    own = pltpu.make_async_copy(blk, home, own_sem.at[1])
    own.start()
    for c in range(4):
        pgram[c] = gram(h * 4 + c)
    send(pgram, ogram, pgs, pgr, partner)
    own.wait()
    for d in range(1, NZ):
        got(home, zr.at[d - 1])

    shared = [0]

    def share(i, j):
        k = shared[0]
        shared[0] += 1
        send(chunk(i, j), chunk(i, j), ps.at[k], pr.at[k], partner)

    def ring_out(row, here, plus, minus):
        send(here, here, as_.at[row, 0], ar.at[row, 0], plus)
        send(here, here, as_.at[row, 1], ar.at[row, 1], minus)

    ring_out(0, chunk(0, 0), to(1, 0), to(-1, 0))
    ring_out(1, chunk(0, 0), to(0, 1), to(0, -1))
    share(0, 0)
    for c in range(4):
        gram_ref[c] = gram(g * 4 + c)
    got(chunk(-1, 0), ar.at[0, 0])
    low = chunk(-1, 0, 0, 4)
    send(low, low, as_.at[0, 2], ar.at[0, 2], to(1, 0))
    ring_out(2, chunk(-1, 0), to(0, 1), to(0, -1))
    share(-1, 0)
    got(chunk(1, 0), ar.at[0, 1])
    high = chunk(1, 0, 4, 4)
    send(high, high, as_.at[0, 3], ar.at[0, 3], to(-1, 0))
    ring_out(3, chunk(1, 0), to(0, 1), to(0, -1))
    share(1, 0)

    def second(row, i):
        got(chunk(i, -1), ar.at[row, 0])
        lo = chunk(i, -1, 0, 4)
        send(lo, lo, as_.at[row, 2], ar.at[row, 2], to(0, 1))
        share(i, -1)
        got(chunk(i, 1), ar.at[row, 1])
        hi = chunk(i, 1, 4, 4)
        send(hi, hi, as_.at[row, 3], ar.at[row, 3], to(0, -1))
        share(i, 1)

    second(1, 0)
    got(chunk(2, 0, 0, 4), ar.at[0, 2])
    got(chunk(2, 0, 4, 4), ar.at[0, 3])
    ring_out(4, chunk(2, 0), to(0, 1), to(0, -1))
    share(2, 0)
    second(2, -1)
    second(3, 1)
    second(4, 2)
    got(ogram, pgr)
    for c in range(4):
        one = jnp.sum(jnp.where(iota((8, 1), 0) == g * 4 + c, denom, 0.0), axis=0, keepdims=True)
        gram_ref[c] = (gram_ref[c] + ogram[c]) / one
    for row, i in ((1, 0), (2, -1), (3, 1), (4, 2)):
        got(chunk(i, 2, 0, 4), ar.at[row, 2])
        got(chunk(i, 2, 4, 4), ar.at[row, 3])
        share(i, 2)
    for k in range(16):
        got(chunk(0, 0, at=pcols), pr.at[k])
    got(sendbuf.at[pl.ds(0, CHIPS - 1)], a2s)
    for c in sent:
        c.wait_send()


def route(embeddings, dest, slot, centroids):
    dma = pltpu.SemaphoreType.DMA
    vm = pltpu.VMEM
    n, d = embeddings.shape
    here = pl.BlockSpec(memory_space=pltpu.VMEM)
    return pl.pallas_call(
        routed,
        out_shape=(jax.ShapeDtypeStruct((NY, NZ, NX, 8, WIDE), BF16), jax.ShapeDtypeStruct((4, SM, SM), F32)),
        in_specs=[here] * 4,
        out_specs=(here, here),
        scratch_shapes=[
            vm((CHIPS, 8, SM), BF16), vm((CHIPS, 8, SM), BF16),
            vm((n, d), BF16), vm((n, 1), jnp.int32), vm((n, 1), jnp.int32),
            vm((4, 4, NZ, 8, 512), F32),
            vm((2, 2, NZ, 8, 512), F32), vm((2, 4, NZ, 8, 512), F32),
            vm((2, 4, 8, 512), F32), vm((2, NZ, 8, 512), F32),
            vm((NZ - 1, 8, 512), F32), vm((8, HALF), BF16), vm((8, HALF), F32), vm((8, HALF), F32),
            vm((4, SM, SM), F32), vm((4, SM, SM), F32),
            dma((2,)), dma, dma, dma((3,)), dma((3,)), dma((6,)), dma((6,)), dma((6,)), dma((6,)),
            dma((7,)), dma((7,)), dma, dma, dma, dma,
            dma((7,)), dma((7,)), dma((5, 4)), dma((5, 4)), dma((16,)), dma((16,)),
        ],
        compiler_params=pltpu.CompilerParams(collective_id=1, has_side_effects=True),
        name="routed",
    )(embeddings, dest, slot, centroids)


BLOCKS = (4, 5, 6, 11, 0, 1, 12, 13, 2, 3, 7, 8, 9, 10)


def permuted(lo_map, hi_map, rank_ref, lo_ref, hi_ref, out_ref, hot):
    del lo_map, hi_map

    @pl.when(pl.program_id(0) == 0)
    def _():
        for b in range(8):
            piece = rank_ref[:, b * 128:(b + 1) * 128].astype(F32)
            eye = iota((128, 128), 0) == iota((128, 128), 1)
            col = jnp.sum(jnp.where(eye, piece, 0.0), axis=1, keepdims=True).astype(jnp.int32)
            hot[b * 128:(b + 1) * 128, :] = (iota((128, 1024), 1) == col).astype(F32).astype(BF16)

    both = jnp.concatenate([lo_ref[...], hi_ref[...]], axis=1)
    out_ref[...] = jnp.dot(hot[...], both, preferred_element_type=F32).astype(BF16)


def permute(table, rank):
    k = table.shape[0]
    return pl.pallas_call(
        permuted,
        grid_spec=pltpu.PrefetchScalarGridSpec(
            num_scalar_prefetch=2,
            grid=(7,),
            in_specs=[
                pl.BlockSpec((1, k), lambda j, lo, hi: (0, 0)),
                pl.BlockSpec((k, 128), lambda j, lo, hi: (0, lo[j])),
                pl.BlockSpec((k, 128), lambda j, lo, hi: (0, hi[j])),
            ],
            out_specs=pl.BlockSpec((k, 256), lambda j, lo, hi: (0, j)),
            scratch_shapes=[pltpu.VMEM((k, k), BF16)],
        ),
        out_shape=jax.ShapeDtypeStruct((k, WIDE), BF16),
        name="permuted",
    )(jnp.array(BLOCKS[0::2], jnp.int32), jnp.array(BLOCKS[1::2], jnp.int32), rank, table, table)


def on_device(embeddings, owner_dest, cluster_slot, cluster_rank, centroids):
    table, moment = route(embeddings, owner_dest, cluster_slot, centroids)
    k = cluster_rank.shape[0]
    shift = permute(table.reshape(k, WIDE), cluster_rank.reshape(1, k))
    return (shift, moment)


def solution(mesh):
    placed = (
        P(("dp", "grp"), None),
        P(("dp", "grp"), None),
        P(("dp", "grp"), None),
        P(),
        P("dp", None),
    )
    return jax.shard_map(
        on_device,
        mesh=mesh,
        in_specs=placed,
        out_specs=(P(), P(("dp", "grp"), None, None)),
        check_vma=False,
    )
```

time: 170 us -> 91 us (0.54)
  waiting for transfers between devices: 55.2 us -> 0 us
  Pallas kernels: 32.2 us -> 86.1 us
  starting transfers between devices: 23.9 us -> 0 us
  matrix products: 14.6 us -> 0 us
  between operations: 14.3 us -> 0.65 us
  other arithmetic: 11.1 us -> 0 us
  local copies, waits for them, and re-layouts: 10.9 us -> 3.92 us
  blocking collectives: 6.71 us -> 0 us
    pallas_call x1 -> x2, Pallas kernels: 32.2 us -> 86.1 us  [the longest x1 76.4 us: route(): pl.pallas_call(routed, out_shape=(jax.ShapeDtypeStruct((NY, NZ, NX, 8, WI...]
    all_to_all x2 -> x0, waiting for transfers between devices: 52.6 us -> none  [the longest x1 46.3 us: on_device(): lax.all_to_all(sent_rows, 'dp', split_axis=0, concat_axis=0, tiled=True)]
    all_to_all x2 -> x0, starting transfers between devices: 23.8 us -> none  [the longest x1 16.3 us: on_device(): lax.all_to_all(sent_ids, 'dp', split_axis=0, concat_axis=0, tiled=True)]
    dot_general x4 -> x0, matrix products: 14.6 us -> none  [the longest x1 7.72 us: on_device(): jnp.dot(pick, table, preferred_element_type=jnp.float32)]
    psum x1 -> x0, blocking collectives: 6.71 us -> none  [on_device(): counts = lax.psum(counts, 'grp')]
    scatter x2 -> x0, local copies, waits for them, and re-layouts: 4.18 us -> none  [pack(): buffer = buffer.at[target].set(values)]
    unnamed x11 -> x5, local copies, waits for them, and re-layouts: 0.03 us -> 3.92 us
    reduce_sum x5 -> x0, other arithmetic: 3.54 us -> none  [the longest x3 2.56 us: residuals(): scale = lax.rsqrt(jnp.mean(part * part, axis=-1, keepdims=True) + 1e-06)]
  transfers between devices with their start and end apart: 4 -> 0, of which waited for: 3 -> 0; matrix products, arithmetic and copies ran while one was open for 11% -> 0% of each run, Pallas kernels for 19% -> 0%
where the time goes in v2:
time: 91 us; the launch traced here: 90.7 us
  Pallas kernels  86.1 us (95%)
  local copies, waits for them, and re-layouts  3.92 us (4%)
    pallas_call x1, Pallas kernels, route(): pl.pallas_call(routed, out_shape=(jax.ShapeDtypeStruct((NY, NZ, NX, 8, WI...  76.4 us
    pallas_call x1, Pallas kernels, permute(): pl.pallas_call(permuted, grid_spec=pltpu.PrefetchScalarGridSpec(num_scala...  9.73 us
    unnamed x5, local copies, waits for them, and re-layouts  3.92 us

profile of v2, /device:TPU:1, one launch (start us, length us, event | category | flops | bytes accessed | tf_op | source)
XLA Modules:
  0.0 90.7 jit_solution(6758554224447205132)
XLA Ops:
  0.6 1.5 %copy.9.dest_ref = s32[256,1]{1,0:T(8,128)} copy(s32[256,1]{0,1:T(1,128)} %param.8) | data formatting | bytes 2048 | tf_op args[1]
  2.1 1.5 %copy.10.slot_ref = s32[256,1]{1,0:T(8,128)} copy(s32[256,1]{0,1:T(1,128)} %param.9) | data formatting | bytes 2048 | tf_op args[2]
  3.6 76.4 %routed.1 = (bf16[4,8,4,8,1792]{4,3,2,1,0:T(8,128)(2,1)}, f32[4,256,256]{2,1,0:T(8,128)}) custom-call(bf16[256,1024]{1,0:T(8,128)(2,1)} %emb_ref.1, s32[256,1]{1,0:T(8,128)} %copy.9.dest_ref, s32[256,1]{1,0:T(8,128)} %copy.10.slot_ref, bf16[8,1024]{1,0:T(8,128)(2,1)} %cent_ref.1), custom_call_target="tpu_custom_call" | custom-call | tf_op jit(solution)/shard_map/routed/pallas_call | solution.py:326
  80.0 0.0 copy-start
  80.0 9.7 %permuted.1 = bf16[1024,1792]{1,0:T(8,128)(2,1)} custom-call(s32[7]{0:T(128)} %constant.4.clone.lo_map, s32[7]{0:T(128)} %constant.5.clone.hi_map, s32[1,1024]{1,0:T(1,128)} %bitcast.4, bf16[1024,1792]{1,0:T(8,128)(2,1)} %bitcast.2, bf16[1024,1792]{1,0:T(8,128)(2,1)} %bitcast.3), custom_call_target="tpu_custom_call" | custom-call | tf_op jit(solution)/shard_map/permuted/pallas_call | solution.py:368
  89.7 0.0 copy-done
  89.7 1.0 %copy.12 = f32[4,256,256]{2,1,0:T(8,128)} copy(f32[4,256,256]{2,1,0:T(8,128)S(1)} %copy-done) | data formatting | bytes 2097152
Async XLA Ops:
  80.0 9.7 %copy-start = (f32[4,256,256]{2,1,0:T(8,128)S(1)}, f32[4,256,256]{2,1,0:T(8,128)}, u32[]{:S(2)}) copy-start(f32[4,256,256]{2,1,0:T(8,128)} %get-tuple-element.9) | copy-start | bytes 3145732

commit v3 on v2

--- a/solution.py
+++ b/solution.py
@@ -35,6 +35,12 @@
     return jnp.sum(jnp.where(eye, col, 0.0), axis=0, keepdims=True)
 
 
+def col_of(row):
+    n = row.shape[1]
+    eye = iota((n, n), 0) == iota((n, n), 1)
+    return jnp.sum(jnp.where(eye, row, 0.0), axis=1, keepdims=True)
+
+
 def scales(rows):
     sq = rows * rows
     s512 = jnp.sum(sq[:, :512], axis=1, keepdims=True)
@@ -42,64 +48,60 @@
     return lax.rsqrt(s512 * (1.0 / 512) + EPS), lax.rsqrt(s1024 * (1.0 / 1024) + EPS)
 
 
-def pack(emb_ref, dest_ref, slot_ref, sendbuf):
-    n = emb_ref.shape[0]
-    dest = dest_ref[...]
-    slot = slot_ref[...]
-    destf = dest.astype(F32)
-    hits = dest == iota((n, CHIPS), 1)
-    lower = (iota((n, n), 1) < iota((n, n), 0)).astype(BF16)
-    before = jnp.dot(lower, hits.astype(F32).astype(BF16), preferred_element_type=F32)
-    pos = jnp.sum(jnp.where(hits, before, 0.0), axis=1, keepdims=True)
-    target = row_of(destf * 8.0 + pos).astype(jnp.int32)
-    destrow = row_of(destf).astype(jnp.int32)
-    s512, s1024 = scales(emb_ref[...].astype(F32))
+def bits(mask):
+    return mask.astype(F32).astype(BF16)
+
+
+def pack(emb_ref, dest, slot, r512, r1024, sendbuf):
+    n = dest.shape[1]
+    hits = iota((CHIPS, n), 0) == dest
+    owner = bits(hits)
+    earlier = bits(iota((n, n), 0) < iota((n, n), 1))
+    before = jnp.dot(owner, earlier, preferred_element_type=F32)
+    pos = jnp.sum(jnp.where(hits, before, 0.0), axis=0, keepdims=True).astype(jnp.int32)
     values = [slot.astype(F32) + 1.0]
-    for s in (s512, s1024):
+    for s in (r512, r1024):
         values += [t.astype(F32) for t in thirds(s)]
-    lane = iota((n, 128), 1)
-    tags = jnp.zeros((n, 128), F32)
-    for q, v in enumerate(values):
-        tags = jnp.where((lane & 15) == q, v, tags)
-    tags = jnp.where((lane >> 4) == pos.astype(jnp.int32), tags, 0.0).astype(BF16)
-    owner = (iota((CHIPS, n), 0) == destrow).astype(F32).astype(BF16)
-    tags = jnp.dot(owner, tags, preferred_element_type=F32)
-    place = (iota((CHIPS * 8, n), 0) == target).astype(F32).astype(BF16)
+    line = iota((128, n), 0)
+    tags = jnp.zeros((128, n), F32)
+    for i, v in enumerate(values):
+        tags = jnp.where((line & 15) == i, v, tags)
+    tags = jnp.where((line >> 4) == pos, tags, 0.0).astype(BF16)
+    tags = lax.dot_general(owner, tags, (((1,), (1,)), ((), ())), preferred_element_type=F32)
+    place = bits(iota((CHIPS * 8, n), 0) == dest * 8 + pos)
     rows = jnp.dot(place, emb_ref[:, :SM], preferred_element_type=F32).reshape(CHIPS, 8, SM)
     wide = jnp.concatenate([tags, jnp.zeros((CHIPS, SM - 128), F32)], axis=1)
     rows = jnp.where(iota((CHIPS, 8, SM), 1) == 6, wide[:, None, :], rows)
     sendbuf[...] = rows.astype(BF16)
 
 
-def whole(embs, dests, slots, g, total):
-    hots, las, lbs = [], [], []
-    for emb_ref, dest_ref, slot_ref in zip(embs, dests, slots):
-        dest = dest_ref[...]
-        xx, zz, yy = dest & 3, (dest >> 2) & 7, dest >> 5
-        a = xx * (1 - g) + yy * g
-        b = yy * (1 - g) + xx * g
-        order = ((a * 4 + b) * 8 + zz) * 8 + slot_ref[...]
-        hots.append(row_of(order.astype(F32)))
-        s512, s1024 = scales(emb_ref[...].astype(F32))
-        gf = g.astype(F32)
-        sa = s512 * (1.0 - gf) + s1024 * gf
-        ca = pl.ds(pl.multiple_of(256 + g * 256, 256), 256)
-        cb = pl.ds(pl.multiple_of(256 + g * 512, 256), 256)
-        las.append(thirds(emb_ref[:, ca].astype(F32) * sa))
-        lbs.append(thirds(emb_ref[:, cb].astype(F32) * s1024))
-    order = jnp.concatenate(hots, axis=1).astype(jnp.int32)
+def order_of(dest, slot, g):
+    xx, zz, yy = dest & 3, (dest >> 2) & 7, dest >> 5
+    a = xx * (1 - g) + yy * g
+    b = yy * (1 - g) + xx * g
+    return ((a * 4 + b) * 8 + zz) * 8 + slot
+
+
+def columns(g):
+    return (pl.ds(pl.multiple_of(256 + g * 256, 256), 256), pl.ds(pl.multiple_of(256 + g * 512, 256), 256))
+
+
+def whole(order, xs, ss, total, add):
     k = 8 * CHIPS
-    hot = (iota((k, order.shape[1]), 0) == order).astype(F32).astype(BF16)
-    for at, parts in ((0, las), (256, lbs)):
-        acc = jnp.zeros((k, 256), F32)
-        for t in range(3):
-            x = jnp.concatenate([p[t] for p in parts], axis=0)
-            acc = acc + jnp.dot(hot, x, preferred_element_type=F32)
-        total[:, :, :, :, at:at + 256] = acc.reshape(4, 4, NZ, 8, 256)
+    hot = bits(iota((k, order.shape[1]), 0) == order)
+    for at, x, s in zip((0, 256), xs, ss):
+        acc = None
+        for t in thirds(x.astype(F32) * s):
+            part = jnp.dot(hot, t, preferred_element_type=F32)
+            acc = part if acc is None else acc + part
+        acc = acc.reshape(4, 4, NZ, 8, 256)
+        if add:
+            acc = acc + total[:, :, :, :, at:at + 256]
+        total[:, :, :, :, at:at + 256] = acc
 
 
 def routed(emb_ref, dest_ref, slot_ref, cent_ref, table_ref, gram_ref,
-           sendbuf, recvbuf, pemb, pdest, pslot, total, half1, full1, half2, full2, zgot, blk, psums, osums,
+           sendbuf, recvbuf, pxa, pxb, info, pinfo, total, half1, full1, half2, full2, zgot, blk, psums, osums,
            pgram, ogram,
            own_sem, a2s, a2r, xs, xr, r1s, r1r, r2s, r2r, z3s, z3r, pss, psr, pgs, pgr,
            zs, zr, as_, ar, ps, pr):
@@ -114,14 +116,27 @@
     pl.semaphore_signal(barrier, inc=1, device_id=partner, device_id_type=MESH)
 
     def chip(d):
-        return (((y + d // 32) % NY) * NZ + (z + (d // 4) % NZ) % NZ) * NX + (x + d % 4) % NX
+        return (((y + 2 + d // 32) % NY) * NZ + (z + 4 + (d // 4) % NZ) % NZ) * NX + (x + 2 + d % 4) % NX
+
+    def others(body):
+        lax.fori_loop(0, 82, body, 0)
+        lax.fori_loop(83, CHIPS, body, 0)
 
     def greet(d, c):
         pl.semaphore_signal(barrier, inc=1, device_id=(chip(d), g), device_id_type=MESH)
         return c
 
-    lax.fori_loop(1, CHIPS, greet, 0)
-    pack(emb_ref, dest_ref, slot_ref, sendbuf)
+    others(greet)
+    dest, slot = dest_ref[...], slot_ref[...]
+    c512, c1024 = scales(emb_ref[...].astype(F32))
+    r512, r1024 = row_of(c512), row_of(c1024)
+    gf = g.astype(F32)
+    info[...] = jnp.zeros_like(info)
+    info[0:1, :] = order_of(dest, slot, h).astype(F32)
+    info[1:2, :] = r512 * gf + r1024 * (1.0 - gf)
+    info[2:3, :] = r1024
+    ca, cb = columns(g)
+    whole(order_of(dest, slot, g), (emb_ref[:, ca], emb_ref[:, cb]), (c512 * (1.0 - gf) + c1024 * gf, c1024), total, False)
     pl.semaphore_wait(barrier, CHIPS)
 
     sent = []
@@ -135,11 +150,17 @@
     def got(ref, sem):
         pltpu.make_async_copy(ref, ref, sem).wait()
 
-    send(emb_ref, pemb, xs.at[0], xr.at[0], partner)
-    send(dest_ref, pdest, xs.at[1], xr.at[1], partner)
-    send(slot_ref, pslot, xs.at[2], xr.at[2], partner)
+    pa, pb = columns(h)
+    send(info, pinfo, xs.at[0], xr.at[0], partner)
+    send(emb_ref.at[:, pa], pxa, xs.at[1], xr.at[1], partner)
+    send(emb_ref.at[:, pb], pxb, xs.at[2], xr.at[2], partner)
+    pack(emb_ref, dest, slot, r512, r1024, sendbuf)
     mine = pltpu.make_async_copy(sendbuf.at[dp], recvbuf.at[dp], own_sem.at[0])
     mine.start()
+    got(pinfo, xr.at[0])
+    got(pxa, xr.at[1])
+    got(pxb, xr.at[2])
+    whole(pinfo[0:1, :].astype(jnp.int32), (pxa[...], pxb[...]), (col_of(pinfo[1:2, :]), col_of(pinfo[2:3, :])), total, True)
 
     def scatter(d, c):
         t = chip(d)
@@ -147,12 +168,6 @@
                                      device_id=(t, g), device_id_type=MESH).start()
         return c
 
-    lax.fori_loop(1, CHIPS, scatter, 0)
-    got(pemb, xr.at[0])
-    got(pdest, xr.at[1])
-    got(pslot, xr.at[2])
-    whole((emb_ref, pemb), (dest_ref, pdest), (slot_ref, pslot), g, total)
-
     def to(i, j):
         yy, xx = (y + 4 + i * g + j * h) % NY, (x + 4 + i * h + j * g) % NX
         return ((yy * NZ + z) * NX + xx, g)
@@ -160,12 +175,13 @@
     p = x * h + y * g
     q = y * h + x * g
 
-    def ring(at, me, lo, hi, half, full, plus, minus, ss, rs):
+    def ring(at, me, lo, hi, half, full, plus, minus, ss, rs, between):
         up, down, far = (me + 1) % 4, (me + 3) % 4, (me + 2) % 4
         send(at(far, lo), half.at[0], ss.at[0], rs.at[0], plus)
         send(at(far, hi), half.at[1], ss.at[1], rs.at[1], minus)
         send(at(up, hi), full.at[0, hi], ss.at[2], rs.at[2], plus)
         send(at(down, lo), full.at[1, lo], ss.at[3], rs.at[3], minus)
+        between()
         got(half.at[0], rs.at[0])
         ref = at(up, lo)
         ref[...] = ref[...] + half[0]
@@ -182,8 +198,10 @@
             ref = at(me, part)
             ref[...] = ref[...] + full[0, part] + full[1, part]
 
-    ring(lambda i, s: total.at[i, s], p, pl.ds(0, 2), pl.ds(2, 2), half1, full1, to(1, 0), to(-1, 0), r1s, r1r)
-    ring(lambda i, s: total.at[p, i, s], q, pl.ds(0, 4), pl.ds(4, 4), half2, full2, to(0, 1), to(0, -1), r2s, r2r)
+    ring(lambda i, s: total.at[i, s], p, pl.ds(0, 2), pl.ds(2, 2), half1, full1, to(1, 0), to(-1, 0), r1s, r1r,
+         lambda: others(scatter))
+    ring(lambda i, s: total.at[p, i, s], q, pl.ds(0, 4), pl.ds(4, 4), half2, full2, to(0, 1), to(0, -1), r2s, r2r,
+         lambda: None)
 
     def along_z(d):
         return ((y * NZ + (z + d) % NZ) * NX + x, g)
@@ -231,11 +249,8 @@
     big = total[p, q, z]
     for d in range(1, NZ):
         big = big + zgot[d - 1]
-    ca = pl.ds(pl.multiple_of(256 + g * 256, 256), 256)
-    cb = pl.ds(pl.multiple_of(256 + g * 512, 256), 256)
     blk[:, 0:256] = ((big[:, :256] - count * cent_ref[:, ca].astype(F32)) / denom).astype(BF16)
     blk[:, 256:512] = ((big[:, 256:] - count * cent_ref[:, cb].astype(F32)) / denom).astype(BF16)
-    gf = g.astype(F32)
     part = jnp.where(gf > 0.5, sums[:, 384:768], sums[:, 0:384])
     blk[:, 512:896] = (part / denom).astype(BF16)
 
@@ -321,7 +336,7 @@
 def route(embeddings, dest, slot, centroids):
     dma = pltpu.SemaphoreType.DMA
     vm = pltpu.VMEM
-    n, d = embeddings.shape
+    n = embeddings.shape[0]
     here = pl.BlockSpec(memory_space=pltpu.VMEM)
     return pl.pallas_call(
         routed,
@@ -330,7 +345,7 @@
         out_specs=(here, here),
         scratch_shapes=[
             vm((CHIPS, 8, SM), BF16), vm((CHIPS, 8, SM), BF16),
-            vm((n, d), BF16), vm((n, 1), jnp.int32), vm((n, 1), jnp.int32),
+            vm((n, 256), BF16), vm((n, 256), BF16), vm((8, n), F32), vm((8, n), F32),
             vm((4, 4, NZ, 8, 512), F32),
             vm((2, 2, NZ, 8, 512), F32), vm((2, 4, NZ, 8, 512), F32),
             vm((2, 4, 8, 512), F32), vm((2, NZ, 8, 512), F32),
@@ -348,7 +363,7 @@
 BLOCKS = (4, 5, 6, 11, 0, 1, 12, 13, 2, 3, 7, 8, 9, 10)
 
 
-def permuted(lo_map, hi_map, rank_ref, lo_ref, hi_ref, out_ref, hot):
+def permuted(lo_map, hi_map, rank_ref, lo_ref, hi_ref, gram_ref, out_ref, moment_ref, hot):
     del lo_map, hi_map
 
     @pl.when(pl.program_id(0) == 0)
@@ -359,11 +374,15 @@
             col = jnp.sum(jnp.where(eye, piece, 0.0), axis=1, keepdims=True).astype(jnp.int32)
             hot[b * 128:(b + 1) * 128, :] = (iota((128, 1024), 1) == col).astype(F32).astype(BF16)
 
+    @pl.when(pl.program_id(0) < 4)
+    def _():
+        moment_ref[...] = gram_ref[...]
+
     both = jnp.concatenate([lo_ref[...], hi_ref[...]], axis=1)
     out_ref[...] = jnp.dot(hot[...], both, preferred_element_type=F32).astype(BF16)
 
 
-def permute(table, rank):
+def permute(table, rank, gram):
     k = table.shape[0]
     return pl.pallas_call(
         permuted,
@@ -374,20 +393,24 @@
                 pl.BlockSpec((1, k), lambda j, lo, hi: (0, 0)),
                 pl.BlockSpec((k, 128), lambda j, lo, hi: (0, lo[j])),
                 pl.BlockSpec((k, 128), lambda j, lo, hi: (0, hi[j])),
+                pl.BlockSpec((1, SM, SM), lambda j, lo, hi: (jnp.minimum(j, 3), 0, 0)),
             ],
-            out_specs=pl.BlockSpec((k, 256), lambda j, lo, hi: (0, j)),
+            out_specs=(
+                pl.BlockSpec((k, 256), lambda j, lo, hi: (0, j)),
+                pl.BlockSpec((1, SM, SM), lambda j, lo, hi: (jnp.minimum(j, 3), 0, 0)),
+            ),
             scratch_shapes=[pltpu.VMEM((k, k), BF16)],
         ),
-        out_shape=jax.ShapeDtypeStruct((k, WIDE), BF16),
+        out_shape=(jax.ShapeDtypeStruct((k, WIDE), BF16), jax.ShapeDtypeStruct(gram.shape, F32)),
         name="permuted",
-    )(jnp.array(BLOCKS[0::2], jnp.int32), jnp.array(BLOCKS[1::2], jnp.int32), rank, table, table)
+    )(jnp.array(BLOCKS[0::2], jnp.int32), jnp.array(BLOCKS[1::2], jnp.int32), rank, table, table, gram)
 
 
 def on_device(embeddings, owner_dest, cluster_slot, cluster_rank, centroids):
-    table, moment = route(embeddings, owner_dest, cluster_slot, centroids)
+    n = embeddings.shape[0]
+    table, gram = route(embeddings, owner_dest.reshape(1, n), cluster_slot.reshape(1, n), centroids)
     k = cluster_rank.shape[0]
-    shift = permute(table.reshape(k, WIDE), cluster_rank.reshape(1, k))
-    return (shift, moment)
+    return permute(table.reshape(k, WIDE), cluster_rank.reshape(1, k), gram)
 
 
 def solution(mesh):

time: 91 us -> 86.6 us (0.952)
  local copies, waits for them, and re-layouts: 3.92 us -> 0 us
    unnamed x5 -> x0, local copies, waits for them, and re-layouts: 3.92 us -> none
where the time goes in v3:
time: 86.6 us; the launch traced here: 86.3 us
  Pallas kernels  85.7 us (99%)
    pallas_call x1, Pallas kernels, route(): pl.pallas_call(routed, out_shape=(jax.ShapeDtypeStruct((NY, NZ, NX, 8, WI...  75.8 us
    pallas_call x1, Pallas kernels, permute(): pl.pallas_call(permuted, grid_spec=pltpu.PrefetchScalarGridSpec(num_scala...  9.9 us

profile of v3, /device:TPU:1, one launch (start us, length us, event | category | flops | bytes accessed | tf_op | source)
XLA Modules:
  0.0 86.3 jit_solution(8498434127411320537)
XLA Ops:
  0.6 75.8 %routed.1 = (bf16[4,8,4,8,1792]{4,3,2,1,0:T(8,128)(2,1)}, f32[4,256,256]{2,1,0:T(8,128)}) custom-call(bf16[256,1024]{1,0:T(8,128)(2,1)} %emb_ref.1, s32[1,256]{1,0:T(1,128)} %bitcast.7, s32[1,256]{1,0:T(1,128)} %bitcast.8, bf16[8,1024]{1,0:T(8,128)(2,1)} %cent_ref.1), custom_call_target="tpu_custom_call" | custom-call | tf_op jit(solution)/shard_map/routed/pallas_call | solution.py:341
  76.4 9.9 %permuted.1 = (bf16[1024,1792]{1,0:T(8,128)(2,1)}, f32[4,256,256]{2,1,0:T(8,128)}) custom-call(s32[7]{0:T(128)} %constant.4.clone.lo_map, s32[7]{0:T(128)} %constant.5.clone.hi_map, s32[1,1024]{1,0:T(1,128)} %bitcast.6, bf16[1024,1792]{1,0:T(8,128)(2,1)} %bitcast.4, bf16[1024,1792]{1,0:T(8,128)(2,1)} %bitcast.5, f32[4,256,256]{2,1,0:T(8,128)} %get-tuple-element.5.gram_ref), custom_call_target="tpu_custom_call" | custom-call | tf_op jit(solution)/shard_map/permuted/pallas_call | solution.py:387

commit v4 on v3

--- a/solution.py
+++ b/solution.py
@@ -100,11 +100,11 @@
         total[:, :, :, :, at:at + 256] = acc
 
 
-def routed(emb_ref, dest_ref, slot_ref, cent_ref, table_ref, gram_ref,
-           sendbuf, recvbuf, pxa, pxb, info, pinfo, total, half1, full1, half2, full2, zgot, blk, psums, osums,
+def routed(emb_ref, dest_ref, slot_ref, cent_ref, rank_ref, table_out, gram_out, hot_out, table_ref, gram_ref, hot_ref,
+           sendbuf, recvbuf, pxa, pxb, info, pinfo, total, half1, full1, full2, zgot, blk, psums, osums,
            pgram, ogram,
            own_sem, a2s, a2r, xs, xr, r1s, r1r, r2s, r2r, z3s, z3r, pss, psr, pgs, pgr,
-           zs, zr, as_, ar, ps, pr):
+           zs, zr, as_, ar, ps, pr, outs):
     dp = lax.axis_index("dp")
     g = lax.axis_index("grp")
     x = dp % NX
@@ -181,7 +181,6 @@
         send(at(far, hi), half.at[1], ss.at[1], rs.at[1], minus)
         send(at(up, hi), full.at[0, hi], ss.at[2], rs.at[2], plus)
         send(at(down, lo), full.at[1, lo], ss.at[3], rs.at[3], minus)
-        between()
         got(half.at[0], rs.at[0])
         ref = at(up, lo)
         ref[...] = ref[...] + half[0]
@@ -190,6 +189,7 @@
         ref = at(down, hi)
         ref[...] = ref[...] + half[1]
         send(ref, full.at[1, hi], ss.at[5], rs.at[5], minus)
+        between()
         got(full.at[0, hi], rs.at[2])
         got(full.at[1, lo], rs.at[3])
         got(full.at[0, lo], rs.at[4])
@@ -200,8 +200,11 @@
 
     ring(lambda i, s: total.at[i, s], p, pl.ds(0, 2), pl.ds(2, 2), half1, full1, to(1, 0), to(-1, 0), r1s, r1r,
          lambda: others(scatter))
-    ring(lambda i, s: total.at[p, i, s], q, pl.ds(0, 4), pl.ds(4, 4), half2, full2, to(0, 1), to(0, -1), r2s, r2r,
-         lambda: None)
+    for i in (2, 1, 3):
+        send(total.at[p, (q + i) % 4], full2.at[i - 1], r2s.at[i - 1], r2r.at[i - 1], to(0, i))
+    for i in (1, 3, 2):
+        got(full2.at[i - 1], r2r.at[i - 1])
+    total[p, q] = total[p, q] + full2[0] + full2[1] + full2[2]
 
     def along_z(d):
         return ((y * NZ + (z + d) % NZ) * NX + x, g)
@@ -269,120 +272,142 @@
     for c in range(4):
         pgram[c] = gram(h * 4 + c)
     send(pgram, ogram, pgs, pgr, partner)
+    for b in range(8):
+        piece = rank_ref[:, b * 128:(b + 1) * 128].astype(F32)
+        col = col_of(piece).astype(jnp.int32)
+        hot_ref[b * 128:(b + 1) * 128, :] = bits(iota((128, 1024), 1) == col)
+    hot_copy = pltpu.make_async_copy(hot_ref, hot_out, outs.at[0])
+    hot_copy.start()
     own.wait()
     for d in range(1, NZ):
         got(home, zr.at[d - 1])
 
-    shared = [0]
+    seen = []
+
+    def keep(yy, xx, at):
+        pltpu.make_async_copy(table_ref.at[yy, :, xx, :, at], table_out.at[yy, :, xx, :, at], outs.at[1]).start()
+
+    def take(k):
+        i, j = seen[k]
+        yy, xx = (y + 4 + i * h + j * g) % NY, (x + 4 + i * g + j * h) % NX
+        got(table_ref.at[yy, :, xx, :, pcols], pr.at[k])
+        keep(yy, xx, pcols)
 
     def share(i, j):
-        k = shared[0]
-        shared[0] += 1
+        k = len(seen)
+        seen.append((i, j))
         send(chunk(i, j), chunk(i, j), ps.at[k], pr.at[k], partner)
-
-    def ring_out(row, here, plus, minus):
-        send(here, here, as_.at[row, 0], ar.at[row, 0], plus)
-        send(here, here, as_.at[row, 1], ar.at[row, 1], minus)
-
-    ring_out(0, chunk(0, 0), to(1, 0), to(-1, 0))
-    ring_out(1, chunk(0, 0), to(0, 1), to(0, -1))
+        keep((y + 4 + i * g + j * h) % NY, (x + 4 + i * h + j * g) % NX, cols)
+        if k >= 5:
+            take(k - 5)
+
+    def out(row, here, along, far):
+        send(here, here, as_.at[row, 0], ar.at[row, 0], along(1))
+        send(here, here, as_.at[row, 1], ar.at[row, 1], along(-1))
+        if far:
+            send(here, here, as_.at[row, 2], ar.at[row, 2], along(2))
+
+    def first(i):
+        return to(i, 0)
+
+    def second(i):
+        return to(0, i)
+
+    out(0, chunk(0, 0), first, True)
+    out(1, chunk(0, 0), second, False)
     share(0, 0)
     for c in range(4):
         gram_ref[c] = gram(g * 4 + c)
     got(chunk(-1, 0), ar.at[0, 0])
-    low = chunk(-1, 0, 0, 4)
-    send(low, low, as_.at[0, 2], ar.at[0, 2], to(1, 0))
-    ring_out(2, chunk(-1, 0), to(0, 1), to(0, -1))
+    out(2, chunk(-1, 0), second, False)
+    got(chunk(1, 0), ar.at[0, 1])
+    out(3, chunk(1, 0), second, False)
     share(-1, 0)
-    got(chunk(1, 0), ar.at[0, 1])
-    high = chunk(1, 0, 4, 4)
-    send(high, high, as_.at[0, 3], ar.at[0, 3], to(-1, 0))
-    ring_out(3, chunk(1, 0), to(0, 1), to(0, -1))
     share(1, 0)
 
-    def second(row, i):
+    def pass_on(row, i):
         got(chunk(i, -1), ar.at[row, 0])
         lo = chunk(i, -1, 0, 4)
         send(lo, lo, as_.at[row, 2], ar.at[row, 2], to(0, 1))
-        share(i, -1)
         got(chunk(i, 1), ar.at[row, 1])
         hi = chunk(i, 1, 4, 4)
         send(hi, hi, as_.at[row, 3], ar.at[row, 3], to(0, -1))
+        share(i, -1)
         share(i, 1)
 
-    second(1, 0)
-    got(chunk(2, 0, 0, 4), ar.at[0, 2])
-    got(chunk(2, 0, 4, 4), ar.at[0, 3])
-    ring_out(4, chunk(2, 0), to(0, 1), to(0, -1))
+    pass_on(1, 0)
+    got(chunk(2, 0), ar.at[0, 2])
+    out(4, chunk(2, 0), second, True)
     share(2, 0)
-    second(2, -1)
-    second(3, 1)
-    second(4, 2)
+    pass_on(2, -1)
+    pass_on(3, 1)
     got(ogram, pgr)
     for c in range(4):
         one = jnp.sum(jnp.where(iota((8, 1), 0) == g * 4 + c, denom, 0.0), axis=0, keepdims=True)
         gram_ref[c] = (gram_ref[c] + ogram[c]) / one
-    for row, i in ((1, 0), (2, -1), (3, 1), (4, 2)):
+    gram_copy = pltpu.make_async_copy(gram_ref, gram_out, outs.at[2])
+    gram_copy.start()
+    for row, i in ((1, 0), (2, -1), (3, 1)):
         got(chunk(i, 2, 0, 4), ar.at[row, 2])
         got(chunk(i, 2, 4, 4), ar.at[row, 3])
         share(i, 2)
-    for k in range(16):
-        got(chunk(0, 0, at=pcols), pr.at[k])
+    for n, i in enumerate((-1, 1, 2)):
+        got(chunk(2, i), ar.at[4, n])
+        share(2, i)
+    for k in range(11, 16):
+        take(k)
+    hot_copy.wait()
+    gram_copy.wait()
+    pltpu.make_async_copy(table_ref, table_out, outs.at[1]).wait()
     got(sendbuf.at[pl.ds(0, CHIPS - 1)], a2s)
     for c in sent:
         c.wait_send()
 
 
-def route(embeddings, dest, slot, centroids):
+def route(embeddings, dest, slot, centroids, rank):
     dma = pltpu.SemaphoreType.DMA
     vm = pltpu.VMEM
     n = embeddings.shape[0]
     here = pl.BlockSpec(memory_space=pltpu.VMEM)
     return pl.pallas_call(
         routed,
-        out_shape=(jax.ShapeDtypeStruct((NY, NZ, NX, 8, WIDE), BF16), jax.ShapeDtypeStruct((4, SM, SM), F32)),
-        in_specs=[here] * 4,
-        out_specs=(here, here),
+        out_shape=(jax.ShapeDtypeStruct((NY, NZ, NX, 8, WIDE), BF16), jax.ShapeDtypeStruct((4, SM, SM), F32),
+                   jax.ShapeDtypeStruct((1024, 1024), BF16)),
+        in_specs=[here] * 5,
+        out_specs=(pl.BlockSpec(memory_space=pl.ANY),) * 3,
         scratch_shapes=[
+            vm((NY, NZ, NX, 8, WIDE), BF16), vm((4, SM, SM), F32), vm((1024, 1024), BF16),
             vm((CHIPS, 8, SM), BF16), vm((CHIPS, 8, SM), BF16),
             vm((n, 256), BF16), vm((n, 256), BF16), vm((8, n), F32), vm((8, n), F32),
             vm((4, 4, NZ, 8, 512), F32),
             vm((2, 2, NZ, 8, 512), F32), vm((2, 4, NZ, 8, 512), F32),
-            vm((2, 4, 8, 512), F32), vm((2, NZ, 8, 512), F32),
+            vm((3, NZ, 8, 512), F32),
             vm((NZ - 1, 8, 512), F32), vm((8, HALF), BF16), vm((8, HALF), F32), vm((8, HALF), F32),
             vm((4, SM, SM), F32), vm((4, SM, SM), F32),
-            dma((2,)), dma, dma, dma((3,)), dma((3,)), dma((6,)), dma((6,)), dma((6,)), dma((6,)),
+            dma((2,)), dma, dma, dma((3,)), dma((3,)), dma((6,)), dma((6,)), dma((3,)), dma((3,)),
             dma((7,)), dma((7,)), dma, dma, dma, dma,
-            dma((7,)), dma((7,)), dma((5, 4)), dma((5, 4)), dma((16,)), dma((16,)),
+            dma((7,)), dma((7,)), dma((5, 4)), dma((5, 4)), dma((16,)), dma((16,)), dma((3,)),
         ],
         compiler_params=pltpu.CompilerParams(collective_id=1, has_side_effects=True),
         name="routed",
-    )(embeddings, dest, slot, centroids)
+    )(embeddings, dest, slot, centroids, rank)
 
 
 BLOCKS = (4, 5, 6, 11, 0, 1, 12, 13, 2, 3, 7, 8, 9, 10)
 
 
-def permuted(lo_map, hi_map, rank_ref, lo_ref, hi_ref, gram_ref, out_ref, moment_ref, hot):
+def permuted(lo_map, hi_map, hot_ref, lo_ref, hi_ref, gram_ref, out_ref, moment_ref):
     del lo_map, hi_map
-
-    @pl.when(pl.program_id(0) == 0)
-    def _():
-        for b in range(8):
-            piece = rank_ref[:, b * 128:(b + 1) * 128].astype(F32)
-            eye = iota((128, 128), 0) == iota((128, 128), 1)
-            col = jnp.sum(jnp.where(eye, piece, 0.0), axis=1, keepdims=True).astype(jnp.int32)
-            hot[b * 128:(b + 1) * 128, :] = (iota((128, 1024), 1) == col).astype(F32).astype(BF16)
 
     @pl.when(pl.program_id(0) < 4)
     def _():
         moment_ref[...] = gram_ref[...]
 
     both = jnp.concatenate([lo_ref[...], hi_ref[...]], axis=1)
-    out_ref[...] = jnp.dot(hot[...], both, preferred_element_type=F32).astype(BF16)
-
-
-def permute(table, rank, gram):
+    out_ref[...] = jnp.dot(hot_ref[...], both, preferred_element_type=F32).astype(BF16)
+
+
+def permute(table, hot, gram):
     k = table.shape[0]
     return pl.pallas_call(
         permuted,
@@ -390,7 +415,7 @@
             num_scalar_prefetch=2,
             grid=(7,),
             in_specs=[
-                pl.BlockSpec((1, k), lambda j, lo, hi: (0, 0)),
+                pl.BlockSpec((k, k), lambda j, lo, hi: (0, 0)),
                 pl.BlockSpec((k, 128), lambda j, lo, hi: (0, lo[j])),
                 pl.BlockSpec((k, 128), lambda j, lo, hi: (0, hi[j])),
                 pl.BlockSpec((1, SM, SM), lambda j, lo, hi: (jnp.minimum(j, 3), 0, 0)),
@@ -399,18 +424,18 @@
                 pl.BlockSpec((k, 256), lambda j, lo, hi: (0, j)),
                 pl.BlockSpec((1, SM, SM), lambda j, lo, hi: (jnp.minimum(j, 3), 0, 0)),
             ),
-            scratch_shapes=[pltpu.VMEM((k, k), BF16)],
         ),
         out_shape=(jax.ShapeDtypeStruct((k, WIDE), BF16), jax.ShapeDtypeStruct(gram.shape, F32)),
         name="permuted",
-    )(jnp.array(BLOCKS[0::2], jnp.int32), jnp.array(BLOCKS[1::2], jnp.int32), rank, table, table, gram)
+    )(jnp.array(BLOCKS[0::2], jnp.int32), jnp.array(BLOCKS[1::2], jnp.int32), hot, table, table, gram)
 
 
 def on_device(embeddings, owner_dest, cluster_slot, cluster_rank, centroids):
     n = embeddings.shape[0]
-    table, gram = route(embeddings, owner_dest.reshape(1, n), cluster_slot.reshape(1, n), centroids)
     k = cluster_rank.shape[0]
-    return permute(table.reshape(k, WIDE), cluster_rank.reshape(1, k), gram)
+    table, gram, hot = route(embeddings, owner_dest.reshape(1, n), cluster_slot.reshape(1, n), centroids,
+                             cluster_rank.reshape(1, k))
+    return permute(table.reshape(k, WIDE), hot, gram)
 
 
 def solution(mesh):

time: 86.6 us -> 82.9 us (0.957)
  Pallas kernels: 85.7 us -> 82 us
    pallas_call x1, Pallas kernels: 75.8 us -> 71.7 us  [route(): pl.pallas_call(routed, out_shape=(jax.ShapeDtypeStruct((NY, NZ, NX, 8, WI...]
where the time goes in v4:
time: 82.9 us; the launch traced here: 82.6 us
  Pallas kernels  82 us (99%)
    pallas_call x1, Pallas kernels, route(): pl.pallas_call(routed, out_shape=(jax.ShapeDtypeStruct((NY, NZ, NX, 8, WI...  71.7 us
    pallas_call x1, Pallas kernels, permute(): pl.pallas_call(permuted, grid_spec=pltpu.PrefetchScalarGridSpec(num_scala...  10.3 us

profile of v4, /device:TPU:1, one launch (start us, length us, event | category | flops | bytes accessed | tf_op | source)
XLA Modules:
  0.0 82.6 jit_solution(132982681985612538)
XLA Ops:
  0.6 71.7 %routed.1 = (bf16[4,8,4,8,1792]{4,3,2,1,0:T(8,128)(2,1)}, f32[4,256,256]{2,1,0:T(8,128)}, bf16[1024,1024]{1,0:T(8,128)(2,1)}) custom-call(bf16[256,1024]{1,0:T(8,128)(2,1)} %emb_ref.1, s32[1,256]{1,0:T(1,128)} %bitcast.7, s32[1,256]{1,0:T(1,128)} %bitcast.8, bf16[8,1024]{1,0:T(8,128)(2,1)} %cent_ref.1, s32[1,1024]{1,0:T(1,128)} %bitcast.6), custom_call_target="tpu_custom_call" | custom-call | tf_op jit(solution)/shard_map/routed/pallas_call | solution.py:372
  72.4 10.3 %permuted.1 = (bf16[1024,1792]{1,0:T(8,128)(2,1)}, f32[4,256,256]{2,1,0:T(8,128)}) custom-call(s32[7]{0:T(128)} %constant.4.clone.lo_map, s32[7]{0:T(128)} %constant.5.clone.hi_map, bf16[1024,1024]{1,0:T(8,128)(2,1)} %get-tuple-element.5.hot_ref, bf16[1024,1792]{1,0:T(8,128)(2,1)} %bitcast.4, bf16[1024,1792]{1,0:T(8,128)(2,1)} %bitcast.5, ...), custom_call_target="tpu_custom_call" | custom-call | tf_op jit(solution)/shard_map/permuted/pallas_call | solution.py:412

commit v5 on v4

--- a/solution.py
+++ b/solution.py
@@ -89,11 +89,9 @@
 def whole(order, xs, ss, total, add):
     k = 8 * CHIPS
     hot = bits(iota((k, order.shape[1]), 0) == order)
+    hot = jnp.concatenate([hot, hot, hot], axis=1)
     for at, x, s in zip((0, 256), xs, ss):
-        acc = None
-        for t in thirds(x.astype(F32) * s):
-            part = jnp.dot(hot, t, preferred_element_type=F32)
-            acc = part if acc is None else acc + part
+        acc = jnp.dot(hot, jnp.concatenate(thirds(x.astype(F32) * s), axis=0), preferred_element_type=F32)
         acc = acc.reshape(4, 4, NZ, 8, 256)
         if add:
             acc = acc + total[:, :, :, :, at:at + 256]
@@ -115,16 +113,28 @@
     barrier = pltpu.get_barrier_semaphore()
     pl.semaphore_signal(barrier, inc=1, device_id=partner, device_id_type=MESH)
 
-    def chip(d):
-        return (((y + 2 + d // 32) % NY) * NZ + (z + 4 + (d // 4) % NZ) % NZ) * NX + (x + 2 + d % 4) % NX
+    xs4 = [(x + 2 + k) % NX for k in range(4)]
 
     def others(body):
-        lax.fori_loop(0, 82, body, 0)
-        lax.fori_loop(83, CHIPS, body, 0)
-
-    def greet(d, c):
-        pl.semaphore_signal(barrier, inc=1, device_id=(chip(d), g), device_id_type=MESH)
-        return c
+        def along(first, last, base, ks):
+            def step(j, c):
+                at = (base + (z + 4 + j) % NZ) * NX
+                for k in ks:
+                    body(at + xs4[k])
+                return c
+            lax.fori_loop(first, last, step, 0)
+
+        for i in range(NY):
+            base = ((y + 2 + i) % NY) * NZ
+            if i == 2:
+                along(0, NZ, base, (0, 1, 3))
+                along(0, 4, base, (2,))
+                along(5, NZ, base, (2,))
+            else:
+                along(0, NZ, base, range(4))
+
+    def greet(t):
+        pl.semaphore_signal(barrier, inc=1, device_id=(t, g), device_id_type=MESH)
 
     others(greet)
     dest, slot = dest_ref[...], slot_ref[...]
@@ -162,11 +172,9 @@
     got(pxb, xr.at[2])
     whole(pinfo[0:1, :].astype(jnp.int32), (pxa[...], pxb[...]), (col_of(pinfo[1:2, :]), col_of(pinfo[2:3, :])), total, True)
 
-    def scatter(d, c):
-        t = chip(d)
+    def scatter(t):
         pltpu.make_async_remote_copy(src_ref=sendbuf.at[t], dst_ref=recvbuf.at[dp], send_sem=a2s, recv_sem=a2r,
                                      device_id=(t, g), device_id_type=MESH).start()
-        return c
 
     def to(i, j):
         yy, xx = (y + 4 + i * g + j * h) % NY, (x + 4 + i * h + j * g) % NX
@@ -393,41 +401,39 @@
     )(embeddings, dest, slot, centroids, rank)
 
 
-BLOCKS = (4, 5, 6, 11, 0, 1, 12, 13, 2, 3, 7, 8, 9, 10)
-
-
-def permuted(lo_map, hi_map, hot_ref, lo_ref, hi_ref, gram_ref, out_ref, moment_ref):
-    del lo_map, hi_map
-
-    @pl.when(pl.program_id(0) < 4)
-    def _():
-        moment_ref[...] = gram_ref[...]
-
-    both = jnp.concatenate([lo_ref[...], hi_ref[...]], axis=1)
-    out_ref[...] = jnp.dot(hot_ref[...], both, preferred_element_type=F32).astype(BF16)
+PARTS = (
+    (0, ((512, 896), (1408, 1536))),
+    (512, ((0, 256),)),
+    (768, ((1536, 1792),)),
+    (1024, ((256, 512),)),
+    (1280, ((896, 1408),)),
+)
+
+
+def permuted(hot_ref, table_ref, gram_ref, out_ref, moment_ref):
+    moment_ref[...] = gram_ref[...]
+    hot = hot_ref[...]
+    for at, spans in PARTS:
+        cols = [table_ref[:, lo:hi] for lo, hi in spans]
+        cols = cols[0] if len(cols) == 1 else jnp.concatenate(cols, axis=1)
+        out_ref[:, at:at + cols.shape[1]] = jnp.dot(hot, cols, preferred_element_type=F32).astype(BF16)
 
 
 def permute(table, hot, gram):
     k = table.shape[0]
+    one = pl.BlockSpec((1, SM, SM), lambda j: (j, 0, 0))
     return pl.pallas_call(
         permuted,
-        grid_spec=pltpu.PrefetchScalarGridSpec(
-            num_scalar_prefetch=2,
-            grid=(7,),
-            in_specs=[
-                pl.BlockSpec((k, k), lambda j, lo, hi: (0, 0)),
-                pl.BlockSpec((k, 128), lambda j, lo, hi: (0, lo[j])),
-                pl.BlockSpec((k, 128), lambda j, lo, hi: (0, hi[j])),
-                pl.BlockSpec((1, SM, SM), lambda j, lo, hi: (jnp.minimum(j, 3), 0, 0)),
-            ],
-            out_specs=(
-                pl.BlockSpec((k, 256), lambda j, lo, hi: (0, j)),
-                pl.BlockSpec((1, SM, SM), lambda j, lo, hi: (jnp.minimum(j, 3), 0, 0)),
-            ),
-        ),
+        grid=(4,),
+        in_specs=[
+            pl.BlockSpec((k // 4, k), lambda j: (j, 0)),
+            pl.BlockSpec((k, WIDE), lambda j: (0, 0)),
+            one,
+        ],
+        out_specs=(pl.BlockSpec((k // 4, WIDE), lambda j: (j, 0)), one),
         out_shape=(jax.ShapeDtypeStruct((k, WIDE), BF16), jax.ShapeDtypeStruct(gram.shape, F32)),
         name="permuted",
-    )(jnp.array(BLOCKS[0::2], jnp.int32), jnp.array(BLOCKS[1::2], jnp.int32), hot, table, table, gram)
+    )(hot, table, gram)
 
 
 def on_device(embeddings, owner_dest, cluster_slot, cluster_rank, centroids):

time: 82.9 us -> 78.6 us (0.948)
  Pallas kernels: 82 us -> 77.8 us
    pallas_call x1, Pallas kernels: 71.7 us -> 69.6 us  [route(): pl.pallas_call(routed, out_shape=(jax.ShapeDtypeStruct((NY, NZ, NX, 8, WI...]
    pallas_call x1, Pallas kernels: 10.3 us -> 8.19 us  [permute(): pl.pallas_call(permuted, grid=(4,), in_specs=[pl.BlockSpec((k // 4, k), l...]
where the time goes in v5:
time: 78.6 us; the launch traced here: 78.5 us
  Pallas kernels  77.8 us (99%)
    pallas_call x1, Pallas kernels, route(): pl.pallas_call(routed, out_shape=(jax.ShapeDtypeStruct((NY, NZ, NX, 8, WI...  69.6 us
    pallas_call x1, Pallas kernels, permute(): pl.pallas_call(permuted, grid=(4,), in_specs=[pl.BlockSpec((k // 4, k), l...  8.19 us

profile of v5, /device:TPU:1, one launch (start us, length us, event | category | flops | bytes accessed | tf_op | source)
XLA Modules:
  0.0 78.5 jit_solution(7062679914160937031)
XLA Ops:
  0.6 69.6 %routed.1 = (bf16[4,8,4,8,1792]{4,3,2,1,0:T(8,128)(2,1)}, f32[4,256,256]{2,1,0:T(8,128)}, bf16[1024,1024]{1,0:T(8,128)(2,1)}) custom-call(bf16[256,1024]{1,0:T(8,128)(2,1)} %emb_ref.1, s32[1,256]{1,0:T(1,128)} %bitcast.6, s32[1,256]{1,0:T(1,128)} %bitcast.7, bf16[8,1024]{1,0:T(8,128)(2,1)} %cent_ref.1, s32[1,1024]{1,0:T(1,128)} %bitcast.5), custom_call_target="tpu_custom_call" | custom-call | tf_op jit(solution)/shard_map/routed/pallas_call | solution.py:380
  70.3 8.2 %permuted.1 = (bf16[1024,1792]{1,0:T(8,128)(2,1)}, f32[4,256,256]{2,1,0:T(8,128)}) custom-call(bf16[1024,1024]{1,0:T(8,128)(2,1)} %get-tuple-element.5.hot_ref, bf16[1024,1792]{1,0:T(8,128)(2,1)} %bitcast.4, f32[4,256,256]{2,1,0:T(8,128)} %get-tuple-element.7.gram_ref), custom_call_target="tpu_custom_call" | custom-call | tf_op jit(solution)/shard_map/permuted/pallas_call | solution.py:425

commit v6 on v5

--- a/solution.py
+++ b/solution.py
@@ -98,11 +98,12 @@
         total[:, :, :, :, at:at + 256] = acc
 
 
-def routed(emb_ref, dest_ref, slot_ref, cent_ref, rank_ref, table_out, gram_out, hot_out, table_ref, gram_ref, hot_ref,
+def routed(emb_in, dest_in, slot_in, cent_in, rank_in, table_ref, gram_out, hot_out,
+           emb_ref, dest_ref, slot_ref, cent_ref, rank_ref, gram_ref, hot_ref,
            sendbuf, recvbuf, pxa, pxb, info, pinfo, total, half1, full1, full2, zgot, blk, psums, osums,
            pgram, ogram,
            own_sem, a2s, a2r, xs, xr, r1s, r1r, r2s, r2r, z3s, z3r, pss, psr, pgs, pgr,
-           zs, zr, as_, ar, ps, pr, outs):
+           zs, zr, as_, ar, ps, pr, outs, ins):
     dp = lax.axis_index("dp")
     g = lax.axis_index("grp")
     x = dp % NX
@@ -110,6 +111,10 @@
     y = dp // (NX * NZ)
     h = 1 - g
     partner = (dp, h)
+    loads = [pltpu.make_async_copy(src, dst, ins.at[i]) for i, (src, dst) in enumerate(
+        ((emb_in, emb_ref), (dest_in, dest_ref), (slot_in, slot_ref), (cent_in, cent_ref), (rank_in, rank_ref)))]
+    for c in loads:
+        c.start()
     barrier = pltpu.get_barrier_semaphore()
     pl.semaphore_signal(barrier, inc=1, device_id=partner, device_id_type=MESH)
 
@@ -137,6 +142,8 @@
         pl.semaphore_signal(barrier, inc=1, device_id=(t, g), device_id_type=MESH)
 
     others(greet)
+    for c in loads:
+        c.wait()
     dest, slot = dest_ref[...], slot_ref[...]
     c512, c1024 = scales(emb_ref[...].astype(F32))
     r512, r1024 = row_of(c512), row_of(c1024)
@@ -292,22 +299,15 @@
 
     seen = []
 
-    def keep(yy, xx, at):
-        pltpu.make_async_copy(table_ref.at[yy, :, xx, :, at], table_out.at[yy, :, xx, :, at], outs.at[1]).start()
-
     def take(k):
         i, j = seen[k]
         yy, xx = (y + 4 + i * h + j * g) % NY, (x + 4 + i * g + j * h) % NX
         got(table_ref.at[yy, :, xx, :, pcols], pr.at[k])
-        keep(yy, xx, pcols)
 
     def share(i, j):
         k = len(seen)
         seen.append((i, j))
         send(chunk(i, j), chunk(i, j), ps.at[k], pr.at[k], partner)
-        keep((y + 4 + i * g + j * h) % NY, (x + 4 + i * h + j * g) % NX, cols)
-        if k >= 5:
-            take(k - 5)
 
     def out(row, here, along, far):
         send(here, here, as_.at[row, 0], ar.at[row, 0], along(1))
@@ -353,7 +353,7 @@
     for c in range(4):
         one = jnp.sum(jnp.where(iota((8, 1), 0) == g * 4 + c, denom, 0.0), axis=0, keepdims=True)
         gram_ref[c] = (gram_ref[c] + ogram[c]) / one
-    gram_copy = pltpu.make_async_copy(gram_ref, gram_out, outs.at[2])
+    gram_copy = pltpu.make_async_copy(gram_ref, gram_out, outs.at[1])
     gram_copy.start()
     for row, i in ((1, 0), (2, -1), (3, 1)):
         got(chunk(i, 2, 0, 4), ar.at[row, 2])
@@ -362,11 +362,10 @@
     for n, i in enumerate((-1, 1, 2)):
         got(chunk(2, i), ar.at[4, n])
         share(2, i)
-    for k in range(11, 16):
+    for k in range(16):
         take(k)
     hot_copy.wait()
     gram_copy.wait()
-    pltpu.make_async_copy(table_ref, table_out, outs.at[1]).wait()
     got(sendbuf.at[pl.ds(0, CHIPS - 1)], a2s)
     for c in sent:
         c.wait_send()
@@ -376,15 +375,15 @@
     dma = pltpu.SemaphoreType.DMA
     vm = pltpu.VMEM
     n = embeddings.shape[0]
-    here = pl.BlockSpec(memory_space=pltpu.VMEM)
     return pl.pallas_call(
         routed,
         out_shape=(jax.ShapeDtypeStruct((NY, NZ, NX, 8, WIDE), BF16), jax.ShapeDtypeStruct((4, SM, SM), F32),
                    jax.ShapeDtypeStruct((1024, 1024), BF16)),
-        in_specs=[here] * 5,
+        in_specs=[pl.BlockSpec(memory_space=pltpu.HBM)] * 5,
         out_specs=(pl.BlockSpec(memory_space=pl.ANY),) * 3,
         scratch_shapes=[
-            vm((NY, NZ, NX, 8, WIDE), BF16), vm((4, SM, SM), F32), vm((1024, 1024), BF16),
+            vm(embeddings.shape, BF16), vm(dest.shape, jnp.int32), vm(slot.shape, jnp.int32), vm(centroids.shape, BF16),
+            vm(rank.shape, jnp.int32), vm((4, SM, SM), F32), vm((1024, 1024), BF16),
             vm((CHIPS, 8, SM), BF16), vm((CHIPS, 8, SM), BF16),
             vm((n, 256), BF16), vm((n, 256), BF16), vm((8, n), F32), vm((8, n), F32),
             vm((4, 4, NZ, 8, 512), F32),
@@ -394,11 +393,11 @@
             vm((4, SM, SM), F32), vm((4, SM, SM), F32),
             dma((2,)), dma, dma, dma((3,)), dma((3,)), dma((6,)), dma((6,)), dma((3,)), dma((3,)),
             dma((7,)), dma((7,)), dma, dma, dma, dma,
-            dma((7,)), dma((7,)), dma((5, 4)), dma((5, 4)), dma((16,)), dma((16,)), dma((3,)),
+            dma((7,)), dma((7,)), dma((5, 4)), dma((5, 4)), dma((16,)), dma((16,)), dma((2,)), dma((5,)),
         ],
-        compiler_params=pltpu.CompilerParams(collective_id=1, has_side_effects=True),
+        compiler_params=pltpu.CompilerParams(collective_id=1, has_side_effects=True, vmem_limit_bytes=32 * 2**20),
         name="routed",
-    )(embeddings, dest, slot, centroids, rank)
+    )(*(pltpu.with_memory_space_constraint(v, pltpu.HBM) for v in (embeddings, dest, slot, centroids, rank)))
 
 
 PARTS = (
@@ -432,6 +431,7 @@
         ],
         out_specs=(pl.BlockSpec((k // 4, WIDE), lambda j: (j, 0)), one),
         out_shape=(jax.ShapeDtypeStruct((k, WIDE), BF16), jax.ShapeDtypeStruct(gram.shape, F32)),
+        compiler_params=pltpu.CompilerParams(vmem_limit_bytes=20 * 2**20),
         name="permuted",
     )(hot, table, gram)
 

time: 78.6 us -> 75.9 us (0.966)
  Pallas kernels: 77.8 us -> 75.2 us
    pallas_call x1, Pallas kernels: 8.19 us -> 5.49 us  [permute(): pl.pallas_call(permuted, grid=(4,), in_specs=[pl.BlockSpec((k // 4, k), l...]
where the time goes in v6:
time: 75.9 us; the launch traced here: 75.8 us
  Pallas kernels  75.2 us (99%)
    pallas_call x1, Pallas kernels, route(): pl.pallas_call(routed, out_shape=(jax.ShapeDtypeStruct((NY, NZ, NX, 8, WI...  69.7 us
    pallas_call x1, Pallas kernels, permute(): pl.pallas_call(permuted, grid=(4,), in_specs=[pl.BlockSpec((k // 4, k), l...  5.49 us

profile of v6, /device:TPU:1, one launch (start us, length us, event | category | flops | bytes accessed | tf_op | source)
XLA Modules:
  0.0 75.8 jit_solution(10647146694593655435)
XLA Ops:
  0.6 69.7 %routed.1 = (bf16[4,8,4,8,1792]{4,3,2,1,0:T(8,128)(2,1)S(1)}, f32[4,256,256]{2,1,0:T(8,128)S(1)}, bf16[1024,1024]{1,0:T(8,128)(2,1)S(1)}) custom-call(bf16[256,1024]{1,0:T(8,128)(2,1)} %emb_in.1, s32[1,256]{1,0:T(1,128)} %bitcast.6, s32[1,256]{1,0:T(1,128)} %bitcast.7, bf16[8,1024]{1,0:T(8,128)(2,1)} %cent_in.1, s32[1,1024]{1,0:T(1,128)} %bitcast.5), custom_call_target="tpu_custom_call" | custom-call | tf_op jit(solution)/shard_map/routed/pallas_call | solution.py:378
  70.3 5.5 %permuted.1 = (bf16[1024,1792]{1,0:T(8,128)(2,1)}, f32[4,256,256]{2,1,0:T(8,128)}) custom-call(bf16[1024,1024]{1,0:T(8,128)(2,1)S(1)} %get-tuple-element.5.hot_ref, bf16[1024,1792]{1,0:T(8,128)(2,1)S(1)} %bitcast.4, f32[4,256,256]{2,1,0:T(8,128)S(1)} %get-tuple-element.7.gram_ref), custom_call_target="tpu_custom_call" | custom-call | tf_op jit(solution)/shard_map/permuted/pallas_call | solution.py:424

commit v7 on v6

--- a/solution.py
+++ b/solution.py
@@ -347,14 +347,14 @@
     got(chunk(2, 0), ar.at[0, 2])
     out(4, chunk(2, 0), second, True)
     share(2, 0)
-    pass_on(2, -1)
-    pass_on(3, 1)
     got(ogram, pgr)
     for c in range(4):
         one = jnp.sum(jnp.where(iota((8, 1), 0) == g * 4 + c, denom, 0.0), axis=0, keepdims=True)
         gram_ref[c] = (gram_ref[c] + ogram[c]) / one
     gram_copy = pltpu.make_async_copy(gram_ref, gram_out, outs.at[1])
     gram_copy.start()
+    pass_on(2, -1)
+    pass_on(3, 1)
     for row, i in ((1, 0), (2, -1), (3, 1)):
         got(chunk(i, 2, 0, 4), ar.at[row, 2])
         got(chunk(i, 2, 4, 4), ar.at[row, 3])
@@ -409,28 +409,32 @@
 )
 
 
-def permuted(hot_ref, table_ref, gram_ref, out_ref, moment_ref):
-    moment_ref[...] = gram_ref[...]
-    hot = hot_ref[...]
-    for at, spans in PARTS:
-        cols = [table_ref[:, lo:hi] for lo, hi in spans]
-        cols = cols[0] if len(cols) == 1 else jnp.concatenate(cols, axis=1)
-        out_ref[:, at:at + cols.shape[1]] = jnp.dot(hot, cols, preferred_element_type=F32).astype(BF16)
+def permuted(hot_ref, table_ref, gram_ref, out_ref, moment_ref, buf, sems):
+    moments = pltpu.make_async_copy(gram_ref, moment_ref, sems.at[4])
+    moments.start()
+    copies = []
+    for j in range(4):
+        rows = pl.ds(j * 256, 256)
+        hot = hot_ref[rows, :]
+        for at, spans in PARTS:
+            cols = [table_ref[:, lo:hi] for lo, hi in spans]
+            cols = cols[0] if len(cols) == 1 else jnp.concatenate(cols, axis=1)
+            buf[rows, at:at + cols.shape[1]] = jnp.dot(hot, cols, preferred_element_type=F32).astype(BF16)
+        copies.append(pltpu.make_async_copy(buf.at[rows], out_ref.at[rows], sems.at[j]))
+        copies[-1].start()
+    for c in copies:
+        c.wait()
+    moments.wait()
 
 
 def permute(table, hot, gram):
     k = table.shape[0]
-    one = pl.BlockSpec((1, SM, SM), lambda j: (j, 0, 0))
     return pl.pallas_call(
         permuted,
-        grid=(4,),
-        in_specs=[
-            pl.BlockSpec((k // 4, k), lambda j: (j, 0)),
-            pl.BlockSpec((k, WIDE), lambda j: (0, 0)),
-            one,
-        ],
-        out_specs=(pl.BlockSpec((k // 4, WIDE), lambda j: (j, 0)), one),
+        in_specs=[pl.BlockSpec(memory_space=pltpu.VMEM)] * 3,
+        out_specs=(pl.BlockSpec(memory_space=pltpu.HBM),) * 2,
         out_shape=(jax.ShapeDtypeStruct((k, WIDE), BF16), jax.ShapeDtypeStruct(gram.shape, F32)),
+        scratch_shapes=[pltpu.VMEM((k, WIDE), BF16), pltpu.SemaphoreType.DMA((5,))],
         compiler_params=pltpu.CompilerParams(vmem_limit_bytes=20 * 2**20),
         name="permuted",
     )(hot, table, gram)

time: 75.9 us -> 75.3 us (level)
  no operation moved by 1% of the time
where the time goes in v7:
time: 75.3 us; the launch traced here: 75.2 us
  Pallas kernels  74.6 us (99%)
    pallas_call x1, Pallas kernels, route(): pl.pallas_call(routed, out_shape=(jax.ShapeDtypeStruct((NY, NZ, NX, 8, WI...  69.7 us
    pallas_call x1, Pallas kernels, permute(): pl.pallas_call(permuted, in_specs=[pl.BlockSpec(memory_space=pltpu.VMEM)]...  4.93 us

profile of v7, /device:TPU:1, one launch (start us, length us, event | category | flops | bytes accessed | tf_op | source)
XLA Modules:
  0.0 75.2 jit_solution(4953319638831681765)
XLA Ops:
  0.6 69.7 %routed.1 = (bf16[4,8,4,8,1792]{4,3,2,1,0:T(8,128)(2,1)S(1)}, f32[4,256,256]{2,1,0:T(8,128)S(1)}, bf16[1024,1024]{1,0:T(8,128)(2,1)S(1)}) custom-call(bf16[256,1024]{1,0:T(8,128)(2,1)} %emb_in.1, s32[1,256]{1,0:T(1,128)} %bitcast.6, s32[1,256]{1,0:T(1,128)} %bitcast.7, bf16[8,1024]{1,0:T(8,128)(2,1)} %cent_in.1, s32[1,1024]{1,0:T(1,128)} %bitcast.5), custom_call_target="tpu_custom_call" | custom-call | tf_op jit(solution)/shard_map/routed/pallas_call | solution.py:378
  70.3 4.9 %permuted.1 = (bf16[1024,1792]{1,0:T(8,128)(2,1)}, f32[4,256,256]{2,1,0:T(8,128)}) custom-call(bf16[1024,1024]{1,0:T(8,128)(2,1)S(1)} %get-tuple-element.5.hot_ref, bf16[1024,1792]{1,0:T(8,128)(2,1)S(1)} %bitcast.4, f32[4,256,256]{2,1,0:T(8,128)S(1)} %get-tuple-element.7.gram_ref), custom_call_target="tpu_custom_call" | custom-call | tf_op jit(solution)/shard_map/permuted/pallas_call | solution.py:432
